TPU v7x, 256 devices: a whole 4x4x8 slice. The times are simulated.
256 devices in a mesh: ep: 32 (over x, z), tp: 8 (over y, core).
Axes of the slice: x: 4, y: 4, z: 8, core: 2. Of those that a mesh axis runs over, the one named last changes fastest.
Arguments:
- attn_out: bfloat16 [8192, 2048], P('ep', 'tp'), may hold values from -6 to 6
- out_proj: bfloat16 [2048, 2048], P('tp'), may hold values from -0.125 to 0.125
- residual: bfloat16 [8192, 2048], P('ep'), may hold values from -40 to 40
- norm_gain: float32 [2048], replicated, may hold values from 0.25 to 1.75
- router: bfloat16 [2048, 64], replicated, may hold values from -0.125 to 0.125
- expert_gate_up: bfloat16 [256, 2, 352, 2048], P(('ep', 'tp')), may hold values from -0.125 to 0.125
- expert_down: bfloat16 [256, 352, 2048], P(('ep', 'tp')), may hold values from -0.15625 to 0.15625
- shared_gate_up: bfloat16 [2, 2816, 2048], P(None, 'tp'), may hold values from -0.125 to 0.125
- shared_down: bfloat16 [2816, 2048], P('tp'), may hold values from -0.109375 to 0.109375
- routes: int32 [8192, 6], P('ep'), may hold values from 0 to 63, all different within a row; in each aligned block of 256 rows (0 to 255, 256 to 511, ...) at most 40 rows name the same one
- live_rows: int32 [32], P('ep'), may hold values from 128 to 256, as said below
- next_gain: float32 [2048], replicated, may hold values from 0.25 to 1.75
Outputs:
- next_stream: bfloat16 [8192, 2048], P('ep', 'tp')
- next_normed: bfloat16 [8192, 2048], P('ep', 'tp')
Inputs may be any that keep to these rules, and one draw needn't show every extreme that they name: `routes`: each row names 6 different experts. Among the 256 rows of one block no expert is named by more than 40 rows, a bound that some block reaches. The live rows of block b are its first live_rows[b] rows; in every draw some block is entirely live.
All inputs are finite; a program needn't handle non-finite values.
Results may differ from a plain program's by a relative error of at most 0.012.
Values may be sent and summed in bfloat16 or wider, within the bound.
A program may use at most 128 MiB of HBM per device.

v0:
```python
import jax
import jax.numpy as jnp
from jax import lax
from jax.sharding import PartitionSpec as P

EXP_DEV = 2


norm_epsilon = 1e-06
routed_scale = 2.446


def slot_table(route_block, live_count, experts, capacity):
    fanout = route_block.shape[1]
    flat_ids = route_block.reshape(-1)
    entry_index = jnp.arange(flat_ids.shape[0], dtype=jnp.int32)
    living = entry_index // fanout < live_count
    one_hot = (
        (flat_ids[:, None] == jnp.arange(experts, dtype=jnp.int32)[None, :]) & living[:, None]
    ).astype(jnp.int32)
    earlier = jnp.cumsum(one_hot, axis=0, dtype=jnp.int32) - one_hot
    position = jnp.sum(earlier * one_hot, axis=1, dtype=jnp.int32)
    slot_index = jnp.where(living, flat_ids * capacity + position, experts * capacity)
    slot_owner = (
        jnp.full((experts * capacity,), -1, jnp.int32).at[slot_index].set(entry_index, mode="drop")
    )
    return (slot_index, living, slot_owner)


def gate_weights(normed, router, route_block):
    logits = jnp.dot(normed, router, preferred_element_type=jnp.float32)
    chosen = jnp.take_along_axis(logits, route_block, axis=1)
    scores = jax.nn.sigmoid(chosen)
    return scores / jnp.sum(scores, axis=1, keepdims=True) * routed_scale


def on_device(
    attn_out,
    out_proj,
    residual,
    norm_gain,
    router,
    expert_gate_up,
    expert_down,
    shared_gate_up,
    shared_down,
    routes,
    live_rows,
    next_gain,
):
    partial_out = jnp.dot(attn_out, out_proj, preferred_element_type=jnp.float32)
    summed = lax.psum(partial_out, "tp")
    stream = (summed + residual.astype(jnp.float32)).astype(jnp.bfloat16)
    stream_wide = stream.astype(jnp.float32)
    normed = (
        stream_wide
        * lax.rsqrt(jnp.mean(stream_wide * stream_wide, axis=1, keepdims=True) + norm_epsilon)
        * norm_gain
    ).astype(jnp.bfloat16)
    width = normed.shape[1]
    tp_count = lax.axis_size("tp")
    ep_count = lax.axis_size("ep")
    width_slice = width // tp_count
    column_start = lax.axis_index("tp") * width_slice
    unit_blocks = tp_count // EXP_DEV
    group = lax.axis_index("tp") // unit_blocks
    experts = router.shape[1]
    fanout = routes.shape[1]
    token_rows = routes.shape[0]
    capacity = token_rows * fanout * 5 // (3 * experts)
    slot_index, living, slot_owner = slot_table(routes, live_rows[0], experts, capacity)
    owners = slot_owner.reshape(ep_count, EXP_DEV, capacity)
    filled = owners >= 0
    source_row = jnp.where(filled, owners // fanout, 0)
    dispatched = jnp.where(filled[:, :, :, None], normed[source_row], jnp.zeros((), jnp.bfloat16))
    rows = lax.dynamic_index_in_dim(
        lax.all_to_all(dispatched, "ep", split_axis=0, concat_axis=0, tiled=True),
        group,
        1,
        keepdims=False,
    )
    gate_proj = jnp.einsum(
        "scd,fd->scf", rows, expert_gate_up[0, 0], preferred_element_type=jnp.float32
    )
    up_proj = jnp.einsum(
        "scd,fd->scf", rows, expert_gate_up[0, 1], preferred_element_type=jnp.float32
    )
    hidden = (jax.nn.silu(gate_proj) * up_proj).astype(jnp.bfloat16)
    produced = jnp.einsum(
        "scf,fd->scd", hidden, expert_down[0], preferred_element_type=jnp.float32
    ).astype(jnp.bfloat16)
    returned = lax.all_to_all(produced, "ep", split_axis=0, concat_axis=0, tiled=True)
    flat_terms = returned.reshape(ep_count * capacity, width)
    living_pairs = living.reshape(token_rows, fanout)
    mine = living_pairs & (routes % EXP_DEV == group)
    position = slot_index.reshape(token_rows, fanout) - routes * capacity
    term_row = jnp.where(mine, routes // EXP_DEV * capacity + position, 0)
    weights = gate_weights(normed, router, routes) * mine.astype(jnp.float32)
    picked = flat_terms[term_row]
    routed_part = jnp.einsum("tkd,tk->td", picked.astype(jnp.float32), weights)
    shared_gate = jnp.einsum(
        "td,fd->tf", normed, shared_gate_up[0], preferred_element_type=jnp.float32
    )
    shared_up = jnp.einsum(
        "td,fd->tf", normed, shared_gate_up[1], preferred_element_type=jnp.float32
    )
    shared_hidden = (jax.nn.silu(shared_gate) * shared_up).astype(jnp.bfloat16)
    shared_part = jnp.dot(shared_hidden, shared_down, preferred_element_type=jnp.float32)
    combined = lax.psum_scatter(
        (routed_part + shared_part).astype(jnp.bfloat16), "tp", scatter_dimension=1, tiled=True
    ).astype(jnp.float32)
    stream_slice = lax.dynamic_slice_in_dim(stream, column_start, width_slice, 1)
    next_stream = (stream_slice.astype(jnp.float32) + combined).astype(jnp.bfloat16)
    next_wide = next_stream.astype(jnp.float32)
    squares = lax.psum(jnp.sum(next_wide * next_wide, axis=1), "tp")
    gain_slice = lax.dynamic_slice_in_dim(next_gain, column_start, width_slice, 0)
    next_normed = (
        next_wide * lax.rsqrt(squares[:, None] / width + norm_epsilon) * gain_slice
    ).astype(jnp.bfloat16)
    return (next_stream, next_normed)


def solution(mesh):
    in_specs = (
        P("ep", "tp"),
        P("tp", None),
        P("ep", None),
        P(),
        P(),
        P(("ep", "tp"), None, None, None),
        P(("ep", "tp"), None, None),
        P(None, "tp", None),
        P("tp", None),
        P("ep", None),
        P("ep"),
        P(),
    )
    out_specs = (P("ep", "tp"), P("ep", "tp"))
    return jax.shard_map(
        on_device, mesh=mesh, in_specs=in_specs, out_specs=out_specs, check_vma=False
    )
```

profile of v0, /device:TPU:1, one launch (start us, length us, event | category | flops | bytes accessed | tf_op | source)
XLA Modules:
  0.0 608.2 jit_solution(8504731297024068242)
XLA Ops:
  7.2 3.1 fusion.76
  11.6 18.1 %reduce-window.6 = s32[64,12,128]{2,1,0:T(8,128)S(1)} reduce-window(s32[64,12,128]{2,1,0:T(8,128)S(1)} %fusion.37, s32[]{:T(128)} %constant.103.clone.1), window={size=1x1x128 pad=0_0x0_0x127_0}, to_apply=%region_1.0 | reduce-window | flops 12484608 | bytes 786436 | tf_op jit(solution)/shard_map/reduce-window
  29.7 0.2 slice.30
  29.9 0.3 copy.44
  30.3 0.2 broadcast_add_fusion
  31.3 6.2 %scatter_custom_fusion = s32[2560]{0:T(1024)S(1)} fusion(s32[1536]{0:T(1024)S(1)} %fusion.67, s32[1536]{0:T(1024)S(1)} %iota.72, s32[]{:T(128)} %constant.107.clone.1), kind=kCustom, calls=%fused_computation.112 | custom fusion | bytes 10244 | tf_op jit(solution)/shard_map/scatter | solution.py:25
  37.7 0.7 ge.27
  38.8 0.6 pad_clamp_fusion
  39.4 44.1 %all-reduce.2.cloned.1.call-done = f32[256,2048]{1,0:T(8,128)} async-done(((f32[256,2048]{1,0:T(8,128)}), f32[256,2048]{1,0:T(8,128)}) %all-reduce.2.cloned.1.call-update) | async-done | bytes 2097168 | tf_op jit(solution)/shard_map/psum | solution.py:52
  83.4 2.3 fusion.7
  85.7 0.3 fusion.9
  86.0 10.9 %gather_fusion = bf16[2560,2048]{1,0:T(8,128)(2,1)} fusion(bf16[256,2048]{1,0:T(8,128)(2,1)S(1)} %fusion.9, s32[3072]{0:T(1024)} %pad_clamp_fusion), kind=kCustom, calls=%fused_computation | custom fusion | bytes 20981760 | tf_op jit(solution)/shard_map/gather | solution.py:75
  97.0 10.0 %broadcast_select_fusion = bf16[32,2,40,2048]{3,2,1,0:T(8,128)(2,1)} fusion(bf16[32,2,40,2048]{3,2,1,0:T(8,128)(2,1)} %bitcast.83, pred[32,2,40]{2,1,0:T(4,128)(4,1)} %ge.27), kind=kLoop, calls=%fused_computation.4 | loop fusion | flops 5242880 | bytes 20974080 | tf_op jit(solution)/shard_map/jit(_where)/select_n | solution.py:75
  106.9 9.7 %all-to-all-start = ((bf16[32,2,40,2048]{3,2,1,0:T(8,128)(2,1)}), bf16[32,2,40,2048]{3,2,1,0:T(8,128)(2,1)}, u32[]{:S(2)}, u32[]{:S(2)}) async-start(bf16[32,2,40,2048]{3,2,1,0:T(8,128)(2,1)} %broadcast_select_fusion), calls=%async_computation | async-start | bytes 20971520 | tf_op jit(solution)/shard_map/all_to_all | solution.py:77
  116.6 232.0 %all-to-all-done = bf16[32,2,40,2048]{3,2,1,0:T(8,128)(2,1)} async-done(((bf16[32,2,40,2048]{3,2,1,0:T(8,128)(2,1)}), bf16[32,2,40,2048]{3,2,1,0:T(8,128)(2,1)}, u32[]{:S(2)}, u32[]{:S(2)}) %all-to-all-start) | async-done | bytes 10485792 | tf_op jit(solution)/shard_map/all_to_all | solution.py:77
  348.6 7.1 %fusion.2 = f32[32,40,352]{2,1,0:T(8,128)} fusion(bf16[32,2,40,2048]{3,2,1,0:T(8,128)(2,1)} %all-to-all-done, s32[]{:T(128)S(6)} %select_n.135, bf16[1,2,352,2048]{3,2,1,0:T(8,128)(2,1)} %param.17), kind=kOutput, calls=%fused_computation.7 | convolution fusion | flops 1845493760 | bytes 8486916 | tf_op jit(solution)/shard_map/scd,fd->scf/dot_general | solution.py:82
  355.7 9.8 %convolution_convert_fusion = bf16[32,40,2048]{2,1,0:T(8,128)(2,1)} fusion(bf16[1,352,2048]{2,1,0:T(8,128)(2,1)S(1)} %copy-done, f32[32,40,352]{2,1,0:T(8,128)} %fusion.2, bf16[32,2,40,2048]{3,2,1,0:T(8,128)(2,1)} %all-to-all-done, s32[]{:T(128)S(6)} %select_n.135, bf16[1,2,352,2048]{3,2,1,0:T(8,128)(2,1)} %param.17), kind=kOutput, calls=%fused_computation.11 | convolution fusion | flops 3696312320 | bytes 15335428 | tf_op jit(solution)/shard_map/scf,fd->scd/dot_general | solution.py:89
  365.5 10.2 %all-to-all-start.1 = ((bf16[32,40,2048]{2,1,0:T(8,128)(2,1)}), bf16[32,40,2048]{2,1,0:T(8,128)(2,1)}, u32[]{:S(2)}, u32[]{:S(2)}) async-start(bf16[32,40,2048]{2,1,0:T(8,128)(2,1)} %convolution_convert_fusion), calls=%async_computation.1 | async-start | bytes 10485760 | tf_op jit(solution)/shard_map/all_to_all | solution.py:92
  375.7 0.2 reduce-scatter.2.cloned.1.call-start
  376.6 0.4 fusion.77
  377.0 12.7 %gather_fusion.2 = f32[1536]{0:T(1024)S(1)} fusion(f32[256,64]{0,1:T(8,128)S(1)} %fusion.77, s32[1536]{0:T(1024)S(1)} %reshape.237), kind=kCustom, calls=%fused_computation.2 | custom fusion | bytes 24576 | tf_op jit(solution)/shard_map/jit(take_along_axis)/gather | solution.py:32
  390.2 2.7 fusion.16
  392.9 99.9 %all-to-all-done.1 = bf16[32,40,2048]{2,1,0:T(8,128)(2,1)} async-done(((bf16[32,40,2048]{2,1,0:T(8,128)(2,1)}), bf16[32,40,2048]{2,1,0:T(8,128)(2,1)}, u32[]{:S(2)}, u32[]{:S(2)}) %all-to-all-start.1) | async-done | bytes 5242912 | tf_op jit(solution)/shard_map/all_to_all | solution.py:92
  492.8 15.8 %gather_fusion.1 = bf16[1536,2048]{1,0:T(8,128)(2,1)} fusion(bf16[1280,2048]{1,0:T(8,128)(2,1)} %bitcast.11, s32[2048]{0:T(1024)S(1)} %pad_clamp_fusion.1), kind=kCustom, calls=%fused_computation.1 | custom fusion | bytes 12589056 | tf_op jit(solution)/shard_map/gather | solution.py:99
  508.7 10.9 %reshape.230 = bf16[256,6,2048]{2,1,0:T(8,128)(2,1)} reshape(bf16[1536,2048]{1,0:T(8,128)(2,1)} %gather_fusion.1) | data formatting | bytes 12582912 | tf_op jit(solution)/shard_map/gather | solution.py:99
  519.6 7.1 %fusion.78 = f32[256,1,2048]{2,1,0:T(1,128)} fusion(bf16[256,6,2048]{2,1,0:T(8,128)(2,1)} %reshape.230, bf16[256,6,1]{1,2,0:T(2,128)(2,1)S(1)} %copy.50), kind=kOutput, calls=%fused_computation.124 | convolution fusion | flops 6291456 | bytes 8391680 | tf_op jit(solution)/shard_map/tkd,tk->td/dot_general | solution.py:100
  526.7 5.9 fusion.6
  532.6 0.8 dynamic_slice.12
  533.4 51.3 %reduce-scatter.2.cloned.1.call-done = bf16[256,256]{1,0:T(8,128)(2,1)} async-done(((bf16[256,2048]{1,0:T(8,128)(2,1)}), bf16[256,256]{1,0:T(8,128)(2,1)}) %reduce-scatter.2.cloned.1.call-update) | async-done | bytes 131088 | tf_op jit(solution)/shard_map/reduce_scatter | solution.py:109
  584.7 1.0 fusion.47
  585.7 14.9 %psum.15 = f32[256]{0:T(256)S(1)} all-reduce(f32[256]{0:T(256)S(1)} %get-tuple-element.2), channel_id=1, replica_groups=mesh['ep'=32,'tp'=8] {'tp'}, use_global_device_ids=true, to_apply=%region_9.10 | all-reduce | flops 256 | bytes 2048 | tf_op jit(solution)/shard_map/psum | solution.py:115
  600.6 0.8 fusion.49
  (51 shorter events, 3.0 us)
Async XLA Ops:
  7.2 348.5 %copy-start = (bf16[1,352,2048]{2,1,0:T(8,128)(2,1)S(1)}, bf16[1,352,2048]{2,1,0:T(8,128)(2,1)}, u32[]{:S(2)}) copy-start(bf16[1,352,2048]{2,1,0:T(8,128)(2,1)} %param.18) | copy-start | bytes 4325380
  7.2 3.2 copy-start.4
  7.2 76.2 %all-reduce.2.cloned.1.call-start = ((), (), s32[]{:S(2)}) async-start(), calls=%async_computation.3 | async-start | bytes 4194304 | tf_op jit(solution)/shard_map/psum | solution.py:52
  83.4 2.3 copy-start.5
  106.9 241.7 %all-to-all-start = ((bf16[32,2,40,2048]{3,2,1,0:T(8,128)(2,1)}), bf16[32,2,40,2048]{3,2,1,0:T(8,128)(2,1)}, u32[]{:S(2)}, u32[]{:S(2)}) async-start(bf16[32,2,40,2048]{3,2,1,0:T(8,128)(2,1)} %broadcast_select_fusion), calls=%async_computation | async-start | bytes 20971520 | tf_op jit(solution)/shard_map/all_to_all | solution.py:77
  365.5 11.1 %copy-start.3 = (bf16[2048,64]{0,1:T(8,128)(2,1)S(1)}, bf16[2048,64]{0,1:T(8,128)(2,1)}, u32[]{:S(2)}) copy-start(bf16[2048,64]{0,1:T(8,128)(2,1)} %param.16) | copy-start | bytes 786436
  365.5 127.3 %all-to-all-start.1 = ((bf16[32,40,2048]{2,1,0:T(8,128)(2,1)}), bf16[32,40,2048]{2,1,0:T(8,128)(2,1)}, u32[]{:S(2)}, u32[]{:S(2)}) async-start(bf16[32,40,2048]{2,1,0:T(8,128)(2,1)} %convolution_convert_fusion), calls=%async_computation.1 | async-start | bytes 10485760 | tf_op jit(solution)/shard_map/all_to_all | solution.py:92
  375.7 209.0 %reduce-scatter.2.cloned.1.call-start = ((), (), s32[]{:S(2)}) async-start(), calls=%async_computation.4 | async-start | bytes 1179648 | tf_op jit(solution)/shard_map/reduce_scatter | solution.py:109
  526.7 74.7 %copy-start.1 = (bf16[1,352,2048]{2,1,0:T(8,128)(2,1)S(1)}, bf16[1,352,2048]{2,1,0:T(8,128)(2,1)}, u32[]{:S(2)}) copy-start(bf16[1,352,2048]{2,1,0:T(8,128)(2,1)} %param.18) | copy-start | bytes 4325380
  585.7 15.7 %copy-start.2 = (bf16[256,256]{1,0:T(8,128)(2,1)}, bf16[256,256]{1,0:T(8,128)(2,1)S(1)}, u32[]{:S(2)}) copy-start(bf16[256,256]{1,0:T(8,128)(2,1)S(1)} %get-tuple-element.3) | copy-start | bytes 393220
Sparse Core Ops, SparseCore 0:
  10.5 72.8 all-reduce.1
  532.7 51.9 reduce-scatter.1
where the time goes:
time: 609 us; the launch traced here: 608 us
  waiting for transfers between devices  427 us (70%)
  local copies, waits for them, and re-layouts  60.9 us (10%)
  matrix products  36.1 us (6%)
  other arithmetic  33.8 us (6%)
  starting transfers between devices  20.1 us (3%)
  between operations  15 us (2%)
  blocking collectives  14.9 us (2%)
    all_to_all x1, waiting for transfers between devices, on_device(): lax.all_to_all(dispatched, 'ep', split_axis=0, concat_axis=0, tiled=True)  232 us
    all_to_all x1, waiting for transfers between devices, on_device(): lax.all_to_all(produced, 'ep', split_axis=0, concat_axis=0, tiled=True)  99.9 us
    reduce_scatter x1, waiting for transfers between devices, on_device(): lax.psum_scatter((routed_part + shared_part).astype(jnp.bfloat16), 'tp',...  51.3 us
    psum x1, waiting for transfers between devices, on_device(): summed = lax.psum(partial_out, 'tp')  44.1 us
    gather x2, local copies, waits for them, and re-layouts, on_device(): picked = flat_terms[term_row]  26.8 us
    another operation x3, other arithmetic  18.4 us
    psum x1, blocking collectives, on_device(): squares = lax.psum(jnp.sum(next_wide * next_wide, axis=1), 'tp')  14.9 us
    gather x5, local copies, waits for them, and re-layouts, gate_weights(): chosen = jnp.take_along_axis(logits, route_block, axis=1)  13.2 us
  transfers between devices with their start and end apart: 4, of which 4 were waited for; matrix products, arithmetic and copies ran while one was open for 8% of the time, Pallas kernels for 0%

commit v1 on v0

v1 whole, which is shorter than its diff:
```python
import jax
import jax.numpy as jnp
from jax import lax
from jax.experimental import pallas as pl
from jax.experimental.pallas import tpu as pltpu
from jax.sharding import PartitionSpec as P

NX, NZ, NY = 4, 8, 4
CAP = 40
PAIRS = {0: (0, 4), 1: (1, 7), 2: (2, 6), 3: (3, 5)}
EPS = 1e-06
SCALE = 2.446
F32 = jnp.float32
BF16 = jnp.bfloat16
MESH = pl.DeviceIdType.MESH


def dot_nn(a, b):
    return lax.dot_general(a, b, (((1,), (0,)), ((), ())), preferred_element_type=F32)


def dot_nt(a, b):
    return lax.dot_general(a, b, (((1,), (1,)), ((), ())), preferred_element_type=F32)


def dot_tn(a, b):
    return lax.dot_general(a, b, (((0,), (0,)), ((), ())), preferred_element_type=F32)


def kernel(
    live_ref, attn_h, proj_h, resid_h, gain_h, router_h, gu_h, dn_h, sgu_h, sdn_h, routes_h, ngain_h,
    out_s, out_n,
    attn, proj, resid, gain, router, gu, dn, sgu, sdn, routes, ngain,
    d2d_s, d2d_r, ys, yr, st, own_acc, ss_s, ss_r,
    code, cz, gt, gz, msel,
    nb, nsib, pmat, wmat, xs, rows, rsib,
    gbuf, hbuf, tsnd, trcv, town, rt,
    sh_own, sh_s, sh_r,
    pb, ysnd, yrcv, rs_s, rs_r, fb_s, fb_r, q_s, q_r,
    load_sem, local_sem, send_sem, recv_sem,
):
    ep = lax.axis_index("ep")
    tp = lax.axis_index("tp")
    x, z = ep // NZ, lax.rem(ep, NZ)
    y, c = tp // 2, lax.rem(tp, 2)
    grp = y // 2
    sc = 1 - c
    T = attn.shape[0]
    W = attn.shape[1]
    FFP = gu.shape[0] // 2
    FF = gu_h.shape[2]

    def at_y(k):
        return lax.rem(y + k, NY)

    def at_z(k):
        return lax.rem(z + k, NZ)

    def at_x(k):
        return lax.rem(x + k, NX)

    def dev(xx=None, zz=None, yy=None, cc=None):
        xx = x if xx is None else xx
        zz = z if zz is None else zz
        yy = y if yy is None else yy
        cc = c if cc is None else cc
        return (xx * NZ + zz, yy * 2 + cc)

    sibling = dev(cc=sc)

    def col(rel, core):
        return pl.multiple_of((at_y(rel) * 2 + core) * W, W)

    copies = []

    def send(src, dst, to):
        i = len(copies)
        cp = pltpu.make_async_remote_copy(
            src_ref=src, dst_ref=dst, send_sem=send_sem.at[i], recv_sem=recv_sem.at[i],
            device_id=to, device_id_type=MESH,
        )
        cp.start()
        copies.append(cp)
        return cp

    loads = []

    def load(src, dst):
        i = len(loads)
        cp = pltpu.make_async_copy(src, dst, load_sem.at[i])
        cp.start()
        loads.append(cp)
        return cp

    locals_ = []

    def local(src, dst):
        i = len(locals_)
        cp = pltpu.make_async_copy(src, dst, local_sem.at[i])
        cp.start()
        locals_.append(cp)
        return cp

    l_attn = load(attn_h, attn)
    l_proj = load(proj_h, proj)
    l_routes = load(routes_h, routes)
    l_resid = load(resid_h.at[:, pl.ds(col(0, c), W)], resid)
    l_gain = load(gain_h, gain)
    l_ngain = load(ngain_h, ngain)
    l_router = load(router_h, router)
    l_sg = load(sgu_h.at[0], sgu.at[pl.ds(0, FF)])
    l_su = load(sgu_h.at[1], sgu.at[pl.ds(FFP, FF)])
    l_sd = load(sdn_h, sdn.at[pl.ds(0, FF)])
    l_g = load(gu_h.at[0, 0], gu.at[pl.ds(0, FF)])
    l_u = load(gu_h.at[0, 1], gu.at[pl.ds(FFP, FF)])
    l_d = load(dn_h.at[0], dn.at[pl.ds(0, FF)])

    peers = [sibling]
    peers += [dev(yy=at_y(k)) for k in (1, 2, 3)]
    peers += [dev(yy=at_y(k), cc=sc) for k in (1, 2, 3)]
    peers += [dev(xx=at_x(k)) for k in (1, 2, 3)]
    peers += [dev(zz=at_z(k)) for k in range(1, NZ)]
    barrier = pltpu.get_barrier_semaphore()
    for peer in peers:
        pl.semaphore_signal(barrier, inc=1, device_id=peer, device_id_type=MESH)

    zpad = jnp.zeros((FFP - FF, gu.shape[1]), BF16)
    for ref in (gu, sgu):
        ref[FF:FFP, :] = zpad
        ref[FFP + FF : 2 * FFP, :] = zpad
    for ref in (dn, sdn):
        ref[FF:FFP, :] = zpad

    l_attn.wait()
    l_proj.wait()
    for rel in (2, 1, 3, 0):
        d2d_s[rel] = dot_nn(attn[...], proj[:, pl.ds(col(rel, sc), W)]).astype(BF16)
    pl.semaphore_wait(barrier, len(peers))
    c_d2d = {rel: send(d2d_s.at[rel], d2d_r.at[rel], sibling) for rel in (2, 1, 3, 0)}
    c_yr = {}
    for rel in (2, 1, 3):
        part = dot_nn(attn[...], proj[:, pl.ds(col(rel, c), W)])
        c_d2d[rel].wait_recv()
        ys[rel - 1] = (part + d2d_r[rel].astype(F32)).astype(BF16)
        c_yr[rel] = send(ys.at[rel - 1], yr.at[rel - 1], dev(yy=at_y(rel)))
    part = dot_nn(attn[...], proj[:, pl.ds(col(0, c), W)])
    c_d2d[0].wait_recv()
    l_resid.wait()
    own_acc[...] = part + d2d_r[0].astype(F32) + resid[...].astype(F32)

    l_routes.wait()
    experts = NX * NZ * 2
    lane_e = lax.broadcasted_iota(jnp.int32, (T, experts), 1)
    chosen = lane_e == routes[:, 0:1]
    for k in range(1, routes.shape[1]):
        chosen = chosen | (lane_e == routes[:, k : k + 1])
    token = lax.broadcasted_iota(jnp.int32, (T, experts), 0)
    alive = token < live_ref[0]
    msel[...] = jnp.where(chosen, 1.0, 0.0)
    active = jnp.where(chosen & alive, 1.0, 0.0).astype(BF16)
    r = lax.broadcasted_iota(jnp.int32, (experts, experts), 0)
    e = lax.broadcasted_iota(jnp.int32, (experts, experts), 1)
    wanted = 2 * ((r & 3) * NZ + (r >> 3)) + ((r >> 2) & 1)
    perm = jnp.where(e == wanted, 1.0, 0.0).astype(BF16)
    act_t = dot_nt(perm, active)
    before = jnp.where(
        lax.broadcasted_iota(jnp.int32, (T, T), 0) < lax.broadcasted_iota(jnp.int32, (T, T), 1), 1.0, 0.0
    ).astype(BF16)
    position = dot_nn(act_t.astype(BF16), before)
    code[...] = jnp.where(act_t > 0.5, position, -1.0)
    c_code = {}
    for k in range(1, NZ):
        c_code[k] = send(
            code.at[pl.ds(pl.multiple_of(at_z(k) * 8, 8), 8)], cz.at[k], dev(zz=at_z(k))
        )
    cz[0] = code[pl.ds(pl.multiple_of(z * 8, 8), 8), :]

    for rel in (1, 3, 2):
        c_yr[rel].wait_recv()
    total = own_acc[...]
    for k in range(3):
        total = total + yr[k].astype(F32)
    st[0] = total.astype(BF16)
    c_st = {rel: send(st.at[0], st.at[rel], dev(yy=at_y(NY - rel))) for rel in (2, 1, 3)}
    for rel in (1, 3, 2):
        c_st[rel].wait_recv()

    sq = None
    for rel in range(4):
        v = st[rel].astype(F32)
        v = v * v
        for k in range(W // 128):
            piece = v[:, k * 128 : (k + 1) * 128]
            sq = piece if sq is None else sq + piece
    ss_s[...] = sq
    c_ss = send(ss_s, ss_r, sibling)
    l_gain.wait()
    c_ss.wait_recv()
    mean = jnp.sum(ss_s[...] + ss_r[...], axis=1, keepdims=True) / (8 * W)
    inv = lax.rsqrt(mean + EPS)

    def gain_row(ref, rel):
        return ref[pl.ds(at_y(rel) * 2 + c, 1), :]

    z_right, z_left = dev(zz=at_z(1)), dev(zz=at_z(NZ - 1))
    y_up, y_down = dev(yy=at_y(1)), dev(yy=at_y(NY - 1))
    ring = {}
    yfw = {}
    for rel in range(4):
        nb[0, rel] = (st[rel].astype(F32) * inv * gain_row(gain, rel)).astype(BF16)
        if rel < 2:
            ring["R", 0, rel] = send(nb.at[0, rel], nb.at[1, rel], z_right)
            ring["L", 0, rel] = send(nb.at[0, rel], nb.at[NZ - 1, rel], z_left)
    c_sib = send(nb.at[0], nsib, sibling)

    def ring_step(s):
        for way, got, nxt in (("R", s + 1, s + 2), ("L", NZ - 1 - s, NZ - 2 - s)):
            for ch in (0, 1):
                if s == 3 and ch != (0 if way == "R" else 1):
                    continue
                ring[way, s, ch].wait_recv()
                if s < 2 or (s == 2 and ch == (0 if way == "R" else 1)):
                    ring[way, s + 1, ch] = send(
                        nb.at[got, ch], nb.at[nxt, ch], z_right if way == "R" else z_left
                    )
                if ch == 0:
                    yfw[got, 3] = send(nb.at[got, 0], nb.at[got, 3], y_up)
                else:
                    yfw[got, 2] = send(nb.at[got, 1], nb.at[got, 2], y_down)

    slot_id = lax.broadcasted_iota(jnp.int32, (CAP, T), 0).astype(F32)
    none = jnp.zeros((CAP, T), F32)

    def build_slots(p):
        a, b = PAIRS[p]
        for k in (a, b):
            if k > 0:
                c_code[k].wait_recv()
        for xp in range(NX):
            ca = cz[a, pl.ds(grp * 4 + xp, 1), :]
            cb = cz[b, pl.ds(grp * 4 + xp, 1), :]
            pa = jnp.where(slot_id == ca, 1.0, 0.0)
            pb_ = jnp.where(slot_id == cb, 1.0, 0.0)
            block = jnp.concatenate(
                [jnp.concatenate([pa, none], axis=1), jnp.concatenate([none, pb_], axis=1)], axis=0
            )
            pmat[p, xp * 2 * CAP : (xp + 1) * 2 * CAP, :] = block.astype(BF16)

    c_x = {}
    l_x = {}
    R = 2 * CAP

    def slots(p):
        a, b = PAIRS[p]
        for rel in range(4):
            picked = dot_nn(pmat[p, :, 0:T], nb[a, rel]) + dot_nn(pmat[p, :, T : 2 * T], nb[b, rel])
            xs[p, :, rel * W : (rel + 1) * W] = picked.astype(BF16)
        here = pl.ds(pl.multiple_of(x * R, R), R)
        for k in (2, 1, 3):
            there = pl.ds(pl.multiple_of(at_x(k) * R, R), R)
            c_x[p, k] = send(xs.at[p, there], rows.at[p, here], dev(xx=at_x(k)))
        l_x[p] = local(xs.at[p, here], rows.at[p, here])

    c_fw = {}

    def forward(p):
        l_x[p].wait()
        for k in (1, 3, 2):
            c_x[p, k].wait_recv()
        c_fw[p] = send(rows.at[p], rsib.at[p], sibling)

    def swiglu(m, own, sib, weights):
        def up(n, carry):
            units = pl.ds(pl.multiple_of(n * 256, 256), 256)
            acc = None
            for rel in range(4):
                t = dot_nt(own(rel), weights[units, pl.ds(col(rel, c), W)])
                acc = t if acc is None else acc + t
            for rel in range(4):
                acc = acc + dot_nt(sib(rel), weights[units, pl.ds(col(rel, sc), W)])
            gbuf[0:m, units] = acc
            return carry

        lax.fori_loop(0, 2 * FFP // 256, up, 0)

        def act(i, carry):
            part = pl.ds(pl.multiple_of(i * (m // 4), 16), m // 4)
            gate = gbuf[part, 0:FFP]
            hbuf[part, :] = (gate / (1.0 + jnp.exp(-gate)) * gbuf[part, FFP : 2 * FFP]).astype(BF16)
            return carry

        lax.fori_loop(0, 4, act, 0)

    c_t = {}

    def expert(p):
        c_fw[p].wait_recv()
        swiglu(
            NX * R,
            lambda rel: rows[p, :, rel * W : (rel + 1) * W],
            lambda rel: rsib[p, :, rel * W : (rel + 1) * W],
            gu,
        )
        for rel in range(4):
            t = dot_nn(hbuf[...], dn[:, pl.ds(col(rel, sc), W)])
            tsnd[p, :, rel * W : (rel + 1) * W] = t.astype(BF16)
        c_t[p] = send(tsnd.at[p], trcv.at[p], sibling)
        for rel in range(4):
            t = dot_nn(hbuf[...], dn[:, pl.ds(col(rel, c), W)])
            town[p, :, rel * W : (rel + 1) * W] = t.astype(BF16)

    c_ret = {}
    l_ret = {}

    def give_back(p):
        c_t[p].wait_recv()
        town[p] = (town[p].astype(F32) + trcv[p].astype(F32)).astype(BF16)
        here = pl.ds(pl.multiple_of(x * R, R), R)
        for k in (2, 1, 3):
            there = pl.ds(pl.multiple_of(at_x(k) * R, R), R)
            c_ret[p, k] = send(town.at[p, there], rt.at[p, here], dev(xx=at_x(k)))
        l_ret[p] = local(town.at[p, here], rt.at[p, here])

    c_y = {}

    def combine(p):
        a, b = PAIRS[p]
        for k in (a, b):
            if k > 0:
                c_gate[k].wait_recv()
        for xp in range(NX):
            ga = gz[a, pl.ds(grp * 4 + xp, 1), :]
            gb = gz[b, pl.ds(grp * 4 + xp, 1), :]
            g2 = jnp.concatenate([ga, gb], axis=1)
            part = slice(xp * R, (xp + 1) * R)
            wmat[part, :] = (pmat[p, part, :].astype(F32) * g2).astype(BF16)
        l_ret[p].wait()
        for k in (1, 3, 2):
            c_ret[p, k].wait_recv()
        for rel in (2, 3, 0, 1):
            for half, k in ((0, a), (1, b)):
                got = dot_tn(wmat[:, half * T : (half + 1) * T], rt[p, :, rel * W : (rel + 1) * W])
                if k == 0:
                    got = got + sh_own[rel].astype(F32) + sh_r[rel].astype(F32)
                if rel < 2:
                    pb[k, rel] = got
                elif rel == 2:
                    ysnd[k, 0] = got.astype(BF16)
                    c_y[k, 1] = send(ysnd.at[k, 0], yrcv.at[k, 1], y_up)
                else:
                    ysnd[k, 1] = got.astype(BF16)
                    c_y[k, 0] = send(ysnd.at[k, 1], yrcv.at[k, 0], y_down)

    for p in (1, 2, 3, 0):
        build_slots(p)
    l_router.wait()
    c_sib.wait_recv()
    logits = None
    for rel in range(4):
        t = dot_nn(nb[0, rel], router[pl.ds(col(rel, c), W), :])
        t = t + dot_nn(nsib[rel], router[pl.ds(col(rel, sc), W), :])
        logits = t if logits is None else logits + t
    scores = msel[...] / (1.0 + jnp.exp(-logits))
    gates = scores / jnp.sum(scores, axis=1, keepdims=True) * SCALE
    gates = jnp.where(alive, gates, 0.0).astype(BF16)
    gt[...] = dot_nt(perm, gates)
    c_gate = {}
    for k in range(1, NZ):
        c_gate[k] = send(gt.at[pl.ds(pl.multiple_of(at_z(k) * 8, 8), 8)], gz.at[k], dev(zz=at_z(k)))
    gz[0] = gt[pl.ds(pl.multiple_of(z * 8, 8), 8), :]

    def wait_y(p):
        for k in PAIRS[p]:
            if k > 0:
                yfw[k, 2].wait_recv()
                yfw[k, 3].wait_recv()

    ring_step(0)
    l_sg.wait()
    l_su.wait()
    l_sd.wait()
    swiglu(T, lambda rel: nb[0, rel], lambda rel: nsib[rel], sgu)
    for rel in range(4):
        sh_s[rel] = dot_nn(hbuf[0:T, :], sdn[:, pl.ds(col(rel, sc), W)]).astype(BF16)
    c_sh = send(sh_s, sh_r, sibling)
    for rel in range(4):
        sh_own[rel] = dot_nn(hbuf[0:T, :], sdn[:, pl.ds(col(rel, c), W)])
    wait_y(1)
    slots(1)
    ring_step(1)
    wait_y(2)
    slots(2)
    forward(1)
    ring_step(2)
    wait_y(3)
    slots(3)
    l_g.wait()
    l_u.wait()
    l_d.wait()
    expert(1)
    ring_step(3)
    wait_y(0)
    slots(0)
    give_back(1)
    forward(2)
    expert(2)
    give_back(2)
    forward(3)
    expert(3)
    give_back(3)
    combine(1)
    forward(0)
    expert(0)
    give_back(0)
    combine(2)
    combine(3)
    c_sh.wait_recv()
    combine(0)

    back = {}

    def value(k, ch):
        c_y[k, ch].wait_recv()
        return pb[k, ch] + yrcv[k, ch].astype(F32)

    for s in range(4):
        for wi, way, k, to in ((0, "L", 4 - s, z_left), (1, "R", 4 + s, z_right)):
            for ch in (0, 1):
                if s == 0 and ch != wi:
                    continue
                if s == 0 and wi == 1:
                    v = value(4, 1)
                else:
                    v = value(k, ch)
                if (way, s - 1, ch) in back:
                    back[way, s - 1, ch].wait_recv()
                    v = v + rs_r[wi, s - 1, ch].astype(F32)
                rs_s[wi, s, ch] = v.astype(BF16)
                back[way, s, ch] = send(rs_s.at[wi, s, ch], rs_r.at[wi, s, ch], to)

    def finish(ch):
        v = value(0, ch)
        for wi, way in ((0, "L"), (1, "R")):
            back[way, 3, ch].wait_recv()
            v = v + rs_r[wi, 3, ch].astype(F32)
        return v

    fb_s[...] = finish(1).astype(BF16)
    c_fb = send(fb_s, fb_r, y_up)
    mine = finish(0) + st[0].astype(F32)
    c_fb.wait_recv()
    nxt = (mine + fb_r[...].astype(F32)).astype(BF16)
    out_s[...] = nxt
    wide = nxt.astype(F32)
    ones = jnp.ones((8, W), F32)
    q_s[...] = lax.dot_general(
        ones, wide * wide, (((1,), (1,)), ((), ())), precision=lax.Precision.HIGHEST, preferred_element_type=F32
    )
    c_q = [send(q_s, q_r.at[0], sibling)]
    for k in (1, 2, 3):
        c_q.append(send(q_s, q_r.at[k], dev(yy=at_y(k))))
        c_q.append(send(q_s, q_r.at[3 + k], dev(yy=at_y(k), cc=sc)))
    l_ngain.wait()
    for cp in c_q:
        cp.wait_recv()
    tot = q_s[...]
    for k in range(7):
        tot = tot + q_r[k]
    inv_t = lax.rsqrt(tot / (8 * W) + EPS)
    inv2 = jnp.transpose(inv_t)[:, 0:1]
    out_n[...] = (wide * inv2 * gain_row(ngain, 0)).astype(BF16)
    for cp in copies:
        cp.wait_send()


N_SEND = 160


def on_device(
    attn_out, out_proj, residual, norm_gain, router, expert_gate_up, expert_down,
    shared_gate_up, shared_down, routes, live_rows, next_gain,
):
    T, W = attn_out.shape
    D = out_proj.shape[1]
    FF = expert_down.shape[1]
    FFP = -(-FF // 128) * 128
    H = D // 2
    R4 = NX * 2 * CAP
    fanout = routes.shape[1]
    vm = pltpu.VMEM
    scratch = [
        vm((T, W), BF16), vm((W, D), BF16), vm((T, W), BF16), vm((8, W), F32), vm((D, 64), BF16),
        vm((2 * FFP, D), BF16), vm((FFP, D), BF16), vm((2 * FFP, D), BF16), vm((FFP, D), BF16),
        vm((T, fanout), jnp.int32), vm((8, W), F32),
        vm((4, T, W), BF16), vm((4, T, W), BF16), vm((3, T, W), BF16), vm((3, T, W), BF16),
        vm((4, T, W), BF16), vm((T, W), F32), vm((T, 128), F32), vm((T, 128), F32),
        vm((64, T), F32), vm((NZ, 8, T), F32), vm((64, T), F32), vm((NZ, 8, T), F32), vm((T, 64), F32),
        vm((NZ, 4, T, W), BF16), vm((4, T, W), BF16), vm((4, R4, 2 * T), BF16), vm((R4, 2 * T), BF16),
        vm((4, R4, H), BF16), vm((4, R4, H), BF16), vm((4, R4, H), BF16),
        vm((R4, 2 * FFP), F32), vm((R4, FFP), BF16),
        vm((4, R4, H), BF16), vm((4, R4, H), BF16), vm((4, R4, H), BF16), vm((4, R4, H), BF16),
        vm((4, T, W), F32), vm((4, T, W), BF16), vm((4, T, W), BF16),
        vm((NZ, 2, T, W), F32), vm((NZ, 2, T, W), BF16), vm((NZ, 2, T, W), BF16),
        vm((2, 4, 2, T, W), BF16), vm((2, 4, 2, T, W), BF16),
        vm((T, W), BF16), vm((T, W), BF16), vm((8, T), F32), vm((7, 8, T), F32),
        pltpu.SemaphoreType.DMA((13,)), pltpu.SemaphoreType.DMA((8,)),
        pltpu.SemaphoreType.DMA((N_SEND,)), pltpu.SemaphoreType.DMA((N_SEND,)),
    ]
    hbm = pl.BlockSpec(memory_space=pl.ANY)
    return pl.pallas_call(
        kernel,
        out_shape=(jax.ShapeDtypeStruct((T, W), BF16), jax.ShapeDtypeStruct((T, W), BF16)),
        in_specs=[pl.BlockSpec(memory_space=pltpu.SMEM)] + [hbm] * 11,
        out_specs=(pl.BlockSpec(memory_space=pltpu.VMEM), pl.BlockSpec(memory_space=pltpu.VMEM)),
        scratch_shapes=scratch,
        compiler_params=pltpu.CompilerParams(
            collective_id=0, has_side_effects=True, vmem_limit_bytes=67043328
        ),
    )(
        live_rows, attn_out, out_proj, residual, norm_gain.reshape(8, W), router, expert_gate_up,
        expert_down, shared_gate_up, shared_down, routes, next_gain.reshape(8, W),
    )


def solution(mesh):
    in_specs = (
        P("ep", "tp"),
        P("tp", None),
        P("ep", None),
        P(),
        P(),
        P(("ep", "tp"), None, None, None),
        P(("ep", "tp"), None, None),
        P(None, "tp", None),
        P("tp", None),
        P("ep", None),
        P("ep"),
        P(),
    )
    out_specs = (P("ep", "tp"), P("ep", "tp"))
    return jax.shard_map(
        on_device, mesh=mesh, in_specs=in_specs, out_specs=out_specs, check_vma=False
    )
```

time: 609 us -> 163 us (0.27)
  waiting for transfers between devices: 427 us -> 0 us
  Pallas kernels: 0 us -> 153 us
  local copies, waits for them, and re-layouts: 60.9 us -> 9.16 us
  matrix products: 36.1 us -> 0 us
  other arithmetic: 33.8 us -> 0 us
  starting transfers between devices: 20.1 us -> 0 us
  blocking collectives: 14.9 us -> 0 us
  between operations: 15 us -> 1.29 us
    all_to_all x2 -> x0, waiting for transfers between devices: 332 us -> none  [the longest x1 232 us: on_device(): lax.all_to_all(dispatched, 'ep', split_axis=0, concat_axis=0, tiled=True)]
    pallas_call x0 -> x1, Pallas kernels: none -> 153 us  [on_device(): pl.pallas_call(kernel, out_shape=(jax.ShapeDtypeStruct((T, W), BF16), jax...]
    reduce_scatter x1 -> x0, waiting for transfers between devices: 51.3 us -> none  [on_device(): lax.psum_scatter((routed_part + shared_part).astype(jnp.bfloat16), 'tp',...]
    gather x8 -> x0, local copies, waits for them, and re-layouts: 50.9 us -> none  [the longest x2 26.8 us: on_device(): picked = flat_terms[term_row]]
    psum x1 -> x0, waiting for transfers between devices: 44.1 us -> none  [on_device(): summed = lax.psum(partial_out, 'tp')]
    dot_general x7 -> x0, matrix products: 36.1 us -> none  [the longest x1 9.78 us: on_device(): jnp.einsum('scf,fd->scd', hidden, expert_down[0], preferred_element_type=...]
    all_to_all x2 -> x0, starting transfers between devices: 19.9 us -> none  [the longest x1 10.2 us: on_device(): lax.all_to_all(produced, 'ep', split_axis=0, concat_axis=0, tiled=True)]
    another operation x3 -> x0, other arithmetic: 18.4 us -> none
  transfers between devices with their start and end apart: 4 -> 0, of which waited for: 4 -> 0; matrix products, arithmetic and copies ran while one was open for 8% -> 0% of each run, Pallas kernels for 0% -> 0%
where the time goes in v1:
time: 163 us
  Pallas kernels  153 us (94%)
  local copies, waits for them, and re-layouts  9.16 us (6%)
    pallas_call x1, Pallas kernels, on_device(): pl.pallas_call(kernel, out_shape=(jax.ShapeDtypeStruct((T, W), BF16), jax...  153 us
    unnamed x4, local copies, waits for them, and re-layouts  6.57 us

profile of v1, /device:TPU:1, one launch (start us, length us, event | category | flops | bytes accessed | tf_op | source)
XLA Modules:
  0.0 163.0 jit_solution(5843502642547894099)
XLA Ops:
  1.3 1.3 reshape.10.gain_h
  2.6 1.3 reshape.11.ngain_h
  3.9 1.5 copy.15.routes_h
  5.4 1.9 %copy.14.router_h = bf16[2048,64]{1,0:T(8,128)(2,1)} copy(bf16[2048,64]{0,1:T(8,128)(2,1)} %param.16) | data formatting | bytes 524288 | tf_op args[4]
  7.3 152.5 %shard_map.131 = (bf16[256,256]{1,0:T(8,128)(2,1)}, bf16[256,256]{1,0:T(8,128)(2,1)}) custom-call(s32[1]{0:T(128)S(6)} %copy.18.live_ref, bf16[256,256]{1,0:T(8,128)(2,1)} %attn_h.1, bf16[256,2048]{1,0:T(8,128)(2,1)} %proj_h.1, bf16[256,2048]{1,0:T(8,128)(2,1)} %resid_h.1, f32[8,256]{1,0:T(8,128)} %reshape.10.gain_h, bf16[2048,64]{1,0:T(8,128)(2,1)} %copy.14.router_h, ...), custom_call_target="tpu_custom_call" | custom-call | tf_op jit(solution)/shard_map/pallas_call | solution.py:510
  159.8 1.6 copy.19
  161.4 1.6 copy.20

commit v2 on v1

v2 whole, which is shorter than its diff:
```python
import jax
import jax.numpy as jnp
from jax import lax
from jax.experimental import pallas as pl
from jax.experimental.pallas import tpu as pltpu
from jax.sharding import PartitionSpec as P

NX, NZ, NY = 4, 8, 4
CAP = 40
CAP_PAD = 48
BLOCKS = {0: (0,), 1: (1, 7), 2: (2, 6), 3: (3, 5), 4: (4,)}
EPS = 1e-06
SCALE = 2.446
F32 = jnp.float32
BF16 = jnp.bfloat16
MESH = pl.DeviceIdType.MESH


def dot_nn(a, b):
    return lax.dot_general(a, b, (((1,), (0,)), ((), ())), preferred_element_type=F32)


def dot_nt(a, b):
    return lax.dot_general(a, b, (((1,), (1,)), ((), ())), preferred_element_type=F32)


def dot_tn(a, b):
    return lax.dot_general(a, b, (((0,), (0,)), ((), ())), preferred_element_type=F32)


def kernel(
    live_ref, attn_h, proj_h, resid_h, gain_h, router_h, gu_h, dn_h, sgu_h, sdn_h, routes_h, ngain_h,
    out_s, out_n,
    attn, proj, resid, gain1, gain, router, gu, dn, sgu, sdn, routes, ngain1, ngain,
    d2d_s, d2d_r, ys, yr, st, own_acc, ss_s, ss_r,
    code, cz, gt, gz,
    nb, nsib, pmat2, pmat1, wmat2, wmat1, xs2, xs1, rows2, rows1, rsib2, rsib1,
    gbuf, hbuf, tsnd2, tsnd1, trcv2, trcv1, town2, town1, rt2, rt1,
    sh_own, sh_s, sh_r,
    pb, ysnd, yrcv, rs_s, rs_r, fb_s, fb_r, q_s, q_r,
    load_sem, local_sem, send_sem, recv_sem,
):
    ep = lax.axis_index("ep")
    tp = lax.axis_index("tp")
    x, z = ep // NZ, lax.rem(ep, NZ)
    y, c = tp // 2, lax.rem(tp, 2)
    grp = y // 2
    sc = 1 - c
    T = attn.shape[0]
    W = attn.shape[1]
    FFP = gu.shape[0] // 2
    FF = gu_h.shape[2]

    def chunk(double, single, p):
        return double.at[p - 1] if 1 <= p <= 3 else single.at[p // 4]

    def per_owner(p):
        return 2 * CAP if 1 <= p <= 3 else CAP_PAD

    def at_y(k):
        return lax.rem(y + k, NY)

    def at_z(k):
        return lax.rem(z + k, NZ)

    def at_x(k):
        return lax.rem(x + k, NX)

    def dev(xx=None, zz=None, yy=None, cc=None):
        xx = x if xx is None else xx
        zz = z if zz is None else zz
        yy = y if yy is None else yy
        cc = c if cc is None else cc
        return (xx * NZ + zz, yy * 2 + cc)

    sibling = dev(cc=sc)

    def col(rel, core):
        return pl.multiple_of((at_y(rel) * 2 + core) * W, W)

    copies = []

    def send(src, dst, to):
        i = len(copies)
        cp = pltpu.make_async_remote_copy(
            src_ref=src, dst_ref=dst, send_sem=send_sem.at[i], recv_sem=recv_sem.at[i],
            device_id=to, device_id_type=MESH,
        )
        cp.start()
        copies.append(cp)
        return cp

    loads = []

    def load(src, dst):
        i = len(loads)
        cp = pltpu.make_async_copy(src, dst, load_sem.at[i])
        cp.start()
        loads.append(cp)
        return cp

    locals_ = []

    def local(src, dst):
        i = len(locals_)
        cp = pltpu.make_async_copy(src, dst, local_sem.at[i])
        cp.start()
        locals_.append(cp)
        return cp

    l_attn = load(attn_h, attn)
    l_proj = load(proj_h, proj)
    l_routes = load(routes_h, routes)
    l_resid = load(resid_h.at[:, pl.ds(col(0, c), W)], resid)
    l_gain = load(gain_h, gain1)
    l_ngain = load(ngain_h, ngain1)
    l_router = load(router_h, router)
    l_sg = load(sgu_h.at[0], sgu.at[pl.ds(0, FF)])
    l_su = load(sgu_h.at[1], sgu.at[pl.ds(FFP, FF)])
    l_sd = load(sdn_h, sdn.at[pl.ds(0, FF)])
    l_g = load(gu_h.at[0, 0], gu.at[pl.ds(0, FF)])
    l_u = load(gu_h.at[0, 1], gu.at[pl.ds(FFP, FF)])
    l_d = load(dn_h.at[0], dn.at[pl.ds(0, FF)])

    peers = [sibling]
    peers += [dev(yy=at_y(k)) for k in (1, 2, 3)]
    peers += [dev(yy=at_y(k), cc=sc) for k in (1, 2, 3)]
    peers += [dev(xx=at_x(k)) for k in (1, 2, 3)]
    peers += [dev(zz=at_z(k)) for k in range(1, NZ)]
    barrier = pltpu.get_barrier_semaphore()
    for peer in peers:
        pl.semaphore_signal(barrier, inc=1, device_id=peer, device_id_type=MESH)

    zpad = jnp.zeros((FFP - FF, gu.shape[1]), BF16)
    for ref in (gu, sgu):
        ref[FF:FFP, :] = zpad
        ref[FFP + FF : 2 * FFP, :] = zpad
    for ref in (dn, sdn):
        ref[FF:FFP, :] = zpad

    l_attn.wait()
    l_proj.wait()
    for rel in (2, 1, 3, 0):
        d2d_s[rel] = dot_nn(attn[...], proj[:, pl.ds(col(rel, sc), W)]).astype(BF16)
    pl.semaphore_wait(barrier, len(peers))
    c_d2d = {rel: send(d2d_s.at[rel], d2d_r.at[rel], sibling) for rel in (2, 1, 3, 0)}
    c_yr = {}
    for rel in (2, 1, 3):
        part = dot_nn(attn[...], proj[:, pl.ds(col(rel, c), W)])
        c_d2d[rel].wait_recv()
        ys[rel - 1] = (part + d2d_r[rel].astype(F32)).astype(BF16)
        c_yr[rel] = send(ys.at[rel - 1], yr.at[rel - 1], dev(yy=at_y(rel)))
    part = dot_nn(attn[...], proj[:, pl.ds(col(0, c), W)])
    c_d2d[0].wait_recv()
    l_resid.wait()
    own_acc[...] = part + d2d_r[0].astype(F32) + resid[...].astype(F32)

    l_routes.wait()
    experts = NX * NZ * 2
    row = lax.broadcasted_iota(jnp.int32, (experts, T), 0)
    alive = lax.broadcasted_iota(jnp.int32, (experts, T), 1) < live_ref[0]
    wanted = 2 * ((row & 3) * NZ + (row >> 3)) + ((row >> 2) & 1)
    chosen = row == routes[0:1, :]
    named = wanted == routes[0:1, :]
    for k in range(1, routes.shape[0]):
        chosen = chosen | (row == routes[k : k + 1, :])
        named = named | (wanted == routes[k : k + 1, :])
    act_t = jnp.where(named & alive, 1.0, 0.0)
    before = jnp.where(
        lax.broadcasted_iota(jnp.int32, (T, T), 0) < lax.broadcasted_iota(jnp.int32, (T, T), 1), 1.0, 0.0
    ).astype(BF16)
    position = dot_nn(act_t.astype(BF16), before)
    code[...] = jnp.where(act_t > 0.5, position, -1.0)
    c_code = {}
    for k in range(1, NZ):
        c_code[k] = send(
            code.at[pl.ds(pl.multiple_of(at_z(k) * 8, 8), 8)], cz.at[k], dev(zz=at_z(k))
        )
    cz[0] = code[pl.ds(pl.multiple_of(z * 8, 8), 8), :]

    for rel in (1, 3, 2):
        c_yr[rel].wait_recv()
    total = own_acc[...]
    for k in range(3):
        total = total + yr[k].astype(F32)
    st[0] = total.astype(BF16)
    ones = jnp.ones((8, W), F32)

    def squares(v):
        return lax.dot_general(
            ones, v * v, (((1,), (1,)), ((), ())), precision=lax.Precision.HIGHEST, preferred_element_type=F32
        )

    def share(src, dst):
        sent = []
        for k in (2, 1, 3):
            sent.append(send(src, dst.at[k], dev(yy=at_y(k))))
            sent.append(send(src, dst.at[3 + k], dev(yy=at_y(k), cc=sc)))
        sent.append(send(src, dst.at[0], sibling))
        return sent

    def inverse(sent, src, dst):
        for cp in sent:
            cp.wait_recv()
        tot = src[...]
        for k in range(7):
            tot = tot + dst[k]
        return jnp.transpose(lax.rsqrt(tot / (8 * W) + EPS))[:, 0:1]

    ss_s[...] = squares(st[0].astype(F32))
    c_ss = share(ss_s, ss_r)
    c_st = {rel: send(st.at[0], st.at[rel], dev(yy=at_y(NY - rel))) for rel in (1, 3, 2)}
    l_gain.wait()
    l_ngain.wait()
    gain[...] = gain1[...].reshape(8, W)
    ngain[...] = ngain1[...].reshape(8, W)
    inv = inverse(c_ss, ss_s, ss_r)

    def gain_row(ref, rel):
        return ref[pl.ds(at_y(rel) * 2 + c, 1), :]

    z_right, z_left = dev(zz=at_z(1)), dev(zz=at_z(NZ - 1))
    y_up, y_down = dev(yy=at_y(1)), dev(yy=at_y(NY - 1))
    ring = {}
    yfw = {}
    for rel in (0, 1, 3, 2):
        if rel > 0:
            c_st[rel].wait_recv()
        nb[0, rel] = (st[rel].astype(F32) * inv * gain_row(gain, rel)).astype(BF16)
        if rel < 2:
            ring["R", 0, rel] = send(nb.at[0, rel], nb.at[1, rel], z_right)
            ring["L", 0, rel] = send(nb.at[0, rel], nb.at[NZ - 1, rel], z_left)
    c_sib = send(nb.at[0], nsib, sibling)

    def ring_step(s):
        for way, got, nxt in (("R", s + 1, s + 2), ("L", NZ - 1 - s, NZ - 2 - s)):
            for ch in (0, 1):
                if s == 3 and ch != (0 if way == "R" else 1):
                    continue
                ring[way, s, ch].wait_recv()
                if s < 2 or (s == 2 and ch == (0 if way == "R" else 1)):
                    ring[way, s + 1, ch] = send(
                        nb.at[got, ch], nb.at[nxt, ch], z_right if way == "R" else z_left
                    )
                if ch == 0:
                    yfw[got, 3] = send(nb.at[got, 0], nb.at[got, 3], y_up)
                else:
                    yfw[got, 2] = send(nb.at[got, 1], nb.at[got, 2], y_down)

    slot2 = lax.broadcasted_iota(jnp.int32, (CAP, T), 0).astype(F32)
    slot1 = lax.broadcasted_iota(jnp.int32, (CAP_PAD, T), 0).astype(F32)
    none = jnp.zeros((CAP, T), F32)

    def code_row(ref, k, xp):
        return ref[k, pl.ds(grp * 4 + xp, 1), :]

    def build_slots(p):
        pm = chunk(pmat2, pmat1, p)
        for k in BLOCKS[p]:
            if k > 0:
                c_code[k].wait_recv()
        R = per_owner(p)
        for xp in range(NX):
            if len(BLOCKS[p]) == 2:
                a, b = BLOCKS[p]
                pa = jnp.where(slot2 == code_row(cz, a, xp), 1.0, 0.0)
                pb_ = jnp.where(slot2 == code_row(cz, b, xp), 1.0, 0.0)
                block = jnp.concatenate(
                    [jnp.concatenate([pa, none], axis=1), jnp.concatenate([none, pb_], axis=1)], axis=0
                )
            else:
                block = jnp.where(slot1 == code_row(cz, BLOCKS[p][0], xp), 1.0, 0.0)
            pm[xp * R : (xp + 1) * R, :] = block.astype(BF16)

    def build_weights(p):
        pm, wm = chunk(pmat2, pmat1, p), chunk(wmat2, wmat1, p)
        for k in BLOCKS[p]:
            if k > 0:
                c_gate[k].wait_recv()
        R = per_owner(p)
        parts = []
        for xp in range(NX):
            g = jnp.concatenate([code_row(gz, k, xp) for k in BLOCKS[p]], axis=1)
            parts.append(pm[xp * R : (xp + 1) * R, :].astype(F32) * g)
        wm[...] = jnp.transpose(jnp.concatenate(parts, axis=0)).astype(BF16)

    c_x = {}
    l_x = {}

    def owner_rows(k, p):
        R = per_owner(p)
        return pl.ds(pl.multiple_of(at_x(k) * R, 16), R)

    def slots(p):
        pm, xs, rows = chunk(pmat2, pmat1, p), chunk(xs2, xs1, p), chunk(rows2, rows1, p)
        for rel in range(4):
            picked = None
            for i, k in enumerate(BLOCKS[p]):
                t = dot_nn(pm[:, i * T : (i + 1) * T], nb[k, rel])
                picked = t if picked is None else picked + t
            xs[:, rel * W : (rel + 1) * W] = picked.astype(BF16)
        for k in (2, 1, 3):
            c_x[p, k] = send(xs.at[owner_rows(k, p)], rows.at[owner_rows(0, p)], dev(xx=at_x(k)))
        l_x[p] = local(xs.at[owner_rows(0, p)], rows.at[owner_rows(0, p)])

    c_fw = {}

    def forward(p):
        l_x[p].wait()
        for k in (1, 3, 2):
            c_x[p, k].wait_recv()
        c_fw[p] = send(chunk(rows2, rows1, p), chunk(rsib2, rsib1, p), sibling)

    def swiglu(m, own, sib, weights):
        def up(n, carry):
            units = pl.ds(pl.multiple_of(n * 256, 256), 256)
            acc = None
            for rel in range(4):
                t = dot_nt(own(rel), weights[units, pl.ds(col(rel, c), W)])
                acc = t if acc is None else acc + t
            for rel in range(4):
                acc = acc + dot_nt(sib(rel), weights[units, pl.ds(col(rel, sc), W)])
            gbuf[0:m, units] = acc
            return carry

        lax.fori_loop(0, 2 * FFP // 256, up, 0)

        def act(i, carry):
            part = pl.ds(pl.multiple_of(i * (m // 4), 16), m // 4)
            gate = gbuf[part, 0:FFP]
            hbuf[part, :] = (gate / (1.0 + jnp.exp(-gate)) * gbuf[part, FFP : 2 * FFP]).astype(BF16)
            return carry

        lax.fori_loop(0, 4, act, 0)

    c_t = {}

    def expert(p):
        rows, rsib = chunk(rows2, rows1, p), chunk(rsib2, rsib1, p)
        tsnd, town = chunk(tsnd2, tsnd1, p), chunk(town2, town1, p)
        m = NX * per_owner(p)
        c_fw[p].wait_recv()
        swiglu(
            m,
            lambda rel: rows[:, rel * W : (rel + 1) * W],
            lambda rel: rsib[:, rel * W : (rel + 1) * W],
            gu,
        )
        for rel in range(4):
            t = dot_nn(hbuf[0:m, :], dn[:, pl.ds(col(rel, sc), W)])
            tsnd[:, rel * W : (rel + 1) * W] = t.astype(BF16)
        c_t[p] = send(tsnd, chunk(trcv2, trcv1, p), sibling)
        for rel in range(4):
            t = dot_nn(hbuf[0:m, :], dn[:, pl.ds(col(rel, c), W)])
            town[:, rel * W : (rel + 1) * W] = t.astype(BF16)

    c_ret = {}
    l_ret = {}

    def give_back(p):
        town, rt = chunk(town2, town1, p), chunk(rt2, rt1, p)
        c_t[p].wait_recv()
        town[...] = (town[...].astype(F32) + chunk(trcv2, trcv1, p)[...].astype(F32)).astype(BF16)
        for k in (2, 1, 3):
            c_ret[p, k] = send(town.at[owner_rows(k, p)], rt.at[owner_rows(0, p)], dev(xx=at_x(k)))
        l_ret[p] = local(town.at[owner_rows(0, p)], rt.at[owner_rows(0, p)])

    c_y = {}

    def combine(p):
        wm, rt = chunk(wmat2, wmat1, p), chunk(rt2, rt1, p)
        l_ret[p].wait()
        for k in (1, 3, 2):
            c_ret[p, k].wait_recv()
        for rel in (2, 3, 1, 0):
            for i, k in enumerate(BLOCKS[p]):
                got = dot_nn(wm[i * T : (i + 1) * T, :], rt[:, rel * W : (rel + 1) * W])
                if k == 0:
                    got = got + sh_own[rel] + sh_r[rel].astype(F32)
                if rel < 2:
                    pb[k, rel] = got
                elif rel == 2:
                    ysnd[k, 0] = got.astype(BF16)
                    c_y[k, 1] = send(ysnd.at[k, 0], yrcv.at[k, 1], y_up)
                else:
                    ysnd[k, 1] = got.astype(BF16)
                    c_y[k, 0] = send(ysnd.at[k, 1], yrcv.at[k, 0], y_down)

    build_slots(0)
    slots(0)
    l_router.wait()
    c_sib.wait_recv()
    logits = None
    for rel in range(4):
        t = dot_nt(router[:, pl.ds(col(rel, c), W)], nb[0, rel])
        t = t + dot_nt(router[:, pl.ds(col(rel, sc), W)], nsib[rel])
        logits = t if logits is None else logits + t
    scores = jnp.where(chosen, 1.0 / (1.0 + jnp.exp(-logits)), 0.0)
    gates = scores / jnp.sum(scores, axis=0, keepdims=True) * SCALE
    gates = jnp.where(alive, gates, 0.0).astype(BF16)
    sel_r = lax.broadcasted_iota(jnp.int32, (experts, experts), 0)
    sel_c = lax.broadcasted_iota(jnp.int32, (experts, experts), 1)
    sel_w = 2 * ((sel_r & 3) * NZ + (sel_r >> 3)) + ((sel_r >> 2) & 1)
    gt[...] = dot_nn(jnp.where(sel_c == sel_w, 1.0, 0.0).astype(BF16), gates)
    c_gate = {}
    for k in range(1, NZ):
        c_gate[k] = send(gt.at[pl.ds(pl.multiple_of(at_z(k) * 8, 8), 8)], gz.at[k], dev(zz=at_z(k)))
    gz[0] = gt[pl.ds(pl.multiple_of(z * 8, 8), 8), :]

    def wait_y(p):
        for k in BLOCKS[p]:
            yfw[k, 2].wait_recv()
            yfw[k, 3].wait_recv()

    for p in (1, 2, 3, 4):
        build_slots(p)
    ring_step(0)
    l_sg.wait()
    l_su.wait()
    l_sd.wait()
    swiglu(T, lambda rel: nb[0, rel], lambda rel: nsib[rel], sgu)
    for rel in range(4):
        sh_s[rel] = dot_nn(hbuf[0:T, :], sdn[:, pl.ds(col(rel, sc), W)]).astype(BF16)
    c_sh = send(sh_s, sh_r, sibling)
    for rel in range(4):
        sh_own[rel] = dot_nn(hbuf[0:T, :], sdn[:, pl.ds(col(rel, c), W)])
    forward(0)
    wait_y(1)
    slots(1)
    ring_step(1)
    for p in (0, 1):
        build_weights(p)
    wait_y(2)
    slots(2)
    l_g.wait()
    l_u.wait()
    l_d.wait()
    expert(0)
    ring_step(2)
    forward(1)
    wait_y(3)
    slots(3)
    expert(1)
    ring_step(3)
    wait_y(4)
    slots(4)
    give_back(0)
    forward(2)
    for p in (2, 3, 4):
        build_weights(p)
    expert(2)
    forward(3)
    expert(3)
    forward(4)
    expert(4)
    give_back(4)
    give_back(3)
    give_back(2)
    give_back(1)
    c_sh.wait_recv()
    combine(0)

    back = {}

    def value(k, ch):
        c_y[k, ch].wait_recv()
        return pb[k, ch] + yrcv[k, ch].astype(F32)

    def pass_on(wi, way, s, ch, k, to):
        v = value(k, ch)
        if (way, s - 1, ch) in back:
            back[way, s - 1, ch].wait_recv()
            v = v + rs_r[wi, s - 1, ch].astype(F32)
        rs_s[wi, s, ch] = v.astype(BF16)
        back[way, s, ch] = send(rs_s.at[wi, s, ch], rs_r.at[wi, s, ch], to)

    combine(4)
    pass_on(0, "L", 0, 0, 4, z_left)
    pass_on(1, "R", 0, 1, 4, z_right)
    for s in (1, 2, 3):
        combine(4 - s)
        for ch in (1, 0):
            pass_on(0, "L", s, ch, 4 - s, z_left)
            pass_on(1, "R", s, ch, 4 + s, z_right)

    def finish(ch):
        v = value(0, ch)
        for wi, way in ((0, "L"), (1, "R")):
            back[way, 3, ch].wait_recv()
            v = v + rs_r[wi, 3, ch].astype(F32)
        return v

    fb_s[...] = finish(1).astype(BF16)
    c_fb = send(fb_s, fb_r, y_up)
    mine = finish(0) + st[0].astype(F32)
    c_fb.wait_recv()
    nxt = (mine + fb_r[...].astype(F32)).astype(BF16)
    out_s[...] = nxt
    wide = nxt.astype(F32)
    q_s[...] = squares(wide)
    inv2 = inverse(share(q_s, q_r), q_s, q_r)
    out_n[...] = (wide * inv2 * gain_row(ngain, 0)).astype(BF16)
    for cp in copies:
        cp.wait_send()


N_SEND = 192


def on_device(
    attn_out, out_proj, residual, norm_gain, router, expert_gate_up, expert_down,
    shared_gate_up, shared_down, routes, live_rows, next_gain,
):
    T, W = attn_out.shape
    D = out_proj.shape[1]
    FF = expert_down.shape[1]
    FFP = -(-FF // 128) * 128
    H = D // 2
    R2, R1 = NX * 2 * CAP, NX * CAP_PAD
    fanout = routes.shape[1]
    vm = pltpu.VMEM
    both = [vm((3, R2, H), BF16), vm((2, R1, H), BF16)]
    scratch = [
        vm((T, W), BF16), vm((W, D), BF16), vm((T, W), BF16), vm((D,), F32), vm((8, W), F32), vm((64, D), BF16),
        vm((2 * FFP, D), BF16), vm((FFP, D), BF16), vm((2 * FFP, D), BF16), vm((FFP, D), BF16),
        vm((fanout, T), jnp.int32), vm((D,), F32), vm((8, W), F32),
        vm((4, T, W), BF16), vm((4, T, W), BF16), vm((3, T, W), BF16), vm((3, T, W), BF16),
        vm((4, T, W), BF16), vm((T, W), F32), vm((8, T), F32), vm((7, 8, T), F32),
        vm((64, T), F32), vm((NZ, 8, T), F32), vm((64, T), F32), vm((NZ, 8, T), F32),
        vm((NZ, 4, T, W), BF16), vm((4, T, W), BF16),
        vm((3, R2, 2 * T), BF16), vm((2, R1, T), BF16), vm((3, 2 * T, R2), BF16), vm((2, T, R1), BF16),
        *both, *both, *both,
        vm((R2, 2 * FFP), F32), vm((R2, FFP), BF16),
        *both, *both, *both, *both,
        vm((4, T, W), F32), vm((4, T, W), BF16), vm((4, T, W), BF16),
        vm((NZ, 2, T, W), F32), vm((NZ, 2, T, W), BF16), vm((NZ, 2, T, W), BF16),
        vm((2, 4, 2, T, W), BF16), vm((2, 4, 2, T, W), BF16),
        vm((T, W), BF16), vm((T, W), BF16), vm((8, T), F32), vm((7, 8, T), F32),
        pltpu.SemaphoreType.DMA((13,)), pltpu.SemaphoreType.DMA((10,)),
        pltpu.SemaphoreType.DMA((N_SEND,)), pltpu.SemaphoreType.DMA((N_SEND,)),
    ]
    hbm = pl.BlockSpec(memory_space=pl.ANY)
    return pl.pallas_call(
        kernel,
        out_shape=(jax.ShapeDtypeStruct((T, W), BF16), jax.ShapeDtypeStruct((T, W), BF16)),
        in_specs=[pl.BlockSpec(memory_space=pltpu.SMEM)] + [hbm] * 11,
        out_specs=(pl.BlockSpec(memory_space=pltpu.VMEM), pl.BlockSpec(memory_space=pltpu.VMEM)),
        scratch_shapes=scratch,
        compiler_params=pltpu.CompilerParams(
            collective_id=0, has_side_effects=True, vmem_limit_bytes=67043328
        ),
    )(
        live_rows, attn_out, out_proj, residual, norm_gain, router.T, expert_gate_up,
        expert_down, shared_gate_up, shared_down, routes.T, next_gain,
    )


def solution(mesh):
    in_specs = (
        P("ep", "tp"),
        P("tp", None),
        P("ep", None),
        P(),
        P(),
        P(("ep", "tp"), None, None, None),
        P(("ep", "tp"), None, None),
        P(None, "tp", None),
        P("tp", None),
        P("ep", None),
        P("ep"),
        P(),
    )
    out_specs = (P("ep", "tp"), P("ep", "tp"))
    return jax.shard_map(
        on_device, mesh=mesh, in_specs=in_specs, out_specs=out_specs, check_vma=False
    )
```

time: 163 us -> 141 us (0.87)
  Pallas kernels: 153 us -> 137 us
  local copies, waits for them, and re-layouts: 9.16 us -> 3.14 us
    pallas_call x1, Pallas kernels: 153 us -> 137 us  [on_device(): pl.pallas_call(kernel, out_shape=(jax.ShapeDtypeStruct((T, W), BF16), jax...]
    unnamed x4 -> x2, local copies, waits for them, and re-layouts: 6.57 us -> 3.14 us
    reshape x2 -> x0, local copies, waits for them, and re-layouts: 2.59 us -> none  [the longest x1 1.3 us: on_device(): norm_gain.reshape(8, W)]
where the time goes in v2:
time: 141 us
  Pallas kernels  137 us (97%)
  local copies, waits for them, and re-layouts  3.14 us (2%)
    pallas_call x1, Pallas kernels, on_device(): pl.pallas_call(kernel, out_shape=(jax.ShapeDtypeStruct((T, W), BF16), jax...  137 us
    unnamed x2, local copies, waits for them, and re-layouts  3.14 us

profile of v2, /device:TPU:1, one launch (start us, length us, event | category | flops | bytes accessed | tf_op | source)
XLA Modules:
  0.0 141.0 jit_solution(351396582207745286)
XLA Ops:
  1.3 136.6 %shard_map.131 = (bf16[256,256]{1,0:T(8,128)(2,1)}, bf16[256,256]{1,0:T(8,128)(2,1)}) custom-call(s32[1]{0:T(128)S(6)} %copy.16.live_ref, bf16[256,256]{1,0:T(8,128)(2,1)} %attn_h.1, bf16[256,2048]{1,0:T(8,128)(2,1)} %proj_h.1, bf16[256,2048]{1,0:T(8,128)(2,1)} %resid_h.1, f32[2048]{0:T(1024)} %gain_h.1, bf16[64,2048]{1,0:T(8,128)(2,1)} %bitcast.2, ...), custom_call_target="tpu_custom_call" | custom-call | tf_op jit(solution)/shard_map/pallas_call | solution.py:543
  137.9 1.6 %copy.17 = bf16[256,256]{1,0:T(8,128)(2,1)} copy(bf16[256,256]{1,0:T(8,128)(2,1)} %get-tuple-element.4) | data formatting | bytes 262144
  139.4 1.6 %copy.18 = bf16[256,256]{1,0:T(8,128)(2,1)} copy(bf16[256,256]{1,0:T(8,128)(2,1)} %get-tuple-element.5) | data formatting | bytes 262144

commit v3 on v2

--- a/solution.py
+++ b/solution.py
@@ -79,16 +79,28 @@
         return pl.multiple_of((at_y(rel) * 2 + core) * W, W)
 
     copies = []
-
-    def send(src, dst, to):
+    fresh = iter(range(N_RECV))
+
+    def group():
+        return next(fresh)
+
+    def send(src, dst, to, sem=None):
         i = len(copies)
+        if i >= N_SEND:
+            copies[i - N_SEND].wait_send()
         cp = pltpu.make_async_remote_copy(
-            src_ref=src, dst_ref=dst, send_sem=send_sem.at[i], recv_sem=recv_sem.at[i],
-            device_id=to, device_id_type=MESH,
+            src_ref=src, dst_ref=dst, send_sem=send_sem.at[i % N_SEND],
+            recv_sem=recv_sem.at[group() if sem is None else sem], device_id=to, device_id_type=MESH,
         )
         cp.start()
         copies.append(cp)
         return cp
+
+    def arrived(sem, size):
+        pltpu.make_async_remote_copy(
+            src_ref=size, dst_ref=size, send_sem=send_sem.at[0], recv_sem=recv_sem.at[sem],
+            device_id=sibling, device_id_type=MESH,
+        ).wait_recv()
 
     loads = []
 
@@ -171,11 +183,9 @@
     ).astype(BF16)
     position = dot_nn(act_t.astype(BF16), before)
     code[...] = jnp.where(act_t > 0.5, position, -1.0)
-    c_code = {}
+    s_code = group()
     for k in range(1, NZ):
-        c_code[k] = send(
-            code.at[pl.ds(pl.multiple_of(at_z(k) * 8, 8), 8)], cz.at[k], dev(zz=at_z(k))
-        )
+        send(code.at[pl.ds(pl.multiple_of(at_z(k) * 8, 8), 8)], cz.at[k], dev(zz=at_z(k)), s_code)
     cz[0] = code[pl.ds(pl.multiple_of(z * 8, 8), 8), :]
 
     for rel in (1, 3, 2):
@@ -192,16 +202,15 @@
         )
 
     def share(src, dst):
-        sent = []
+        sem = group()
         for k in (2, 1, 3):
-            sent.append(send(src, dst.at[k], dev(yy=at_y(k))))
-            sent.append(send(src, dst.at[3 + k], dev(yy=at_y(k), cc=sc)))
-        sent.append(send(src, dst.at[0], sibling))
-        return sent
-
-    def inverse(sent, src, dst):
-        for cp in sent:
-            cp.wait_recv()
+            send(src, dst.at[k], dev(yy=at_y(k)), sem)
+            send(src, dst.at[3 + k], dev(yy=at_y(k), cc=sc), sem)
+        send(src, dst.at[0], sibling, sem)
+        return sem
+
+    def inverse(sem, src, dst):
+        arrived(sem, dst)
         tot = src[...]
         for k in range(7):
             tot = tot + dst[k]
@@ -214,6 +223,10 @@
     l_ngain.wait()
     gain[...] = gain1[...].reshape(8, W)
     ngain[...] = ngain1[...].reshape(8, W)
+    slot1 = lax.broadcasted_iota(jnp.int32, (CAP_PAD, T), 0).astype(F32)
+    for xp in range(NX):
+        own_code = cz[0, pl.ds(grp * 4 + xp, 1), :]
+        pmat1[0, xp * CAP_PAD : (xp + 1) * CAP_PAD, :] = jnp.where(slot1 == own_code, 1.0, 0.0).astype(BF16)
     inv = inverse(c_ss, ss_s, ss_r)
 
     def gain_row(ref, rel):
@@ -223,18 +236,23 @@
     y_up, y_down = dev(yy=at_y(1)), dev(yy=at_y(NY - 1))
     ring = {}
     yfw = {}
-    for rel in (0, 1, 3, 2):
+
+    def normalise(rel):
         if rel > 0:
             c_st[rel].wait_recv()
         nb[0, rel] = (st[rel].astype(F32) * inv * gain_row(gain, rel)).astype(BF16)
         if rel < 2:
             ring["R", 0, rel] = send(nb.at[0, rel], nb.at[1, rel], z_right)
             ring["L", 0, rel] = send(nb.at[0, rel], nb.at[NZ - 1, rel], z_left)
-    c_sib = send(nb.at[0], nsib, sibling)
+
+    normalise(0)
+    normalise(1)
+
+    s_yfw = {p: group() for p in (1, 2, 3, 4)}
 
     def ring_step(s):
-        for way, got, nxt in (("R", s + 1, s + 2), ("L", NZ - 1 - s, NZ - 2 - s)):
-            for ch in (0, 1):
+        for ch in (0, 1):
+            for way, got, nxt in (("R", s + 1, s + 2), ("L", NZ - 1 - s, NZ - 2 - s)):
                 if s == 3 and ch != (0 if way == "R" else 1):
                     continue
                 ring[way, s, ch].wait_recv()
@@ -243,9 +261,9 @@
                         nb.at[got, ch], nb.at[nxt, ch], z_right if way == "R" else z_left
                     )
                 if ch == 0:
-                    yfw[got, 3] = send(nb.at[got, 0], nb.at[got, 3], y_up)
+                    send(nb.at[got, 0], nb.at[got, 3], y_up, s_yfw[s + 1])
                 else:
-                    yfw[got, 2] = send(nb.at[got, 1], nb.at[got, 2], y_down)
+                    send(nb.at[got, 1], nb.at[got, 2], y_down, s_yfw[s + 1])
 
     slot2 = lax.broadcasted_iota(jnp.int32, (CAP, T), 0).astype(F32)
     slot1 = lax.broadcasted_iota(jnp.int32, (CAP_PAD, T), 0).astype(F32)
@@ -256,9 +274,6 @@
 
     def build_slots(p):
         pm = chunk(pmat2, pmat1, p)
-        for k in BLOCKS[p]:
-            if k > 0:
-                c_code[k].wait_recv()
         R = per_owner(p)
         for xp in range(NX):
             if len(BLOCKS[p]) == 2:
@@ -274,9 +289,6 @@
 
     def build_weights(p):
         pm, wm = chunk(pmat2, pmat1, p), chunk(wmat2, wmat1, p)
-        for k in BLOCKS[p]:
-            if k > 0:
-                c_gate[k].wait_recv()
         R = per_owner(p)
         parts = []
         for xp in range(NX):
@@ -284,32 +296,34 @@
             parts.append(pm[xp * R : (xp + 1) * R, :].astype(F32) * g)
         wm[...] = jnp.transpose(jnp.concatenate(parts, axis=0)).astype(BF16)
 
-    c_x = {}
+    s_x = {p: group() for p in range(5)}
     l_x = {}
 
     def owner_rows(k, p):
         R = per_owner(p)
         return pl.ds(pl.multiple_of(at_x(k) * R, 16), R)
 
-    def slots(p):
+    def slots(p, half):
         pm, xs, rows = chunk(pmat2, pmat1, p), chunk(xs2, xs1, p), chunk(rows2, rows1, p)
-        for rel in range(4):
+        for rel in (2 * half, 2 * half + 1):
             picked = None
             for i, k in enumerate(BLOCKS[p]):
                 t = dot_nn(pm[:, i * T : (i + 1) * T], nb[k, rel])
                 picked = t if picked is None else picked + t
             xs[:, rel * W : (rel + 1) * W] = picked.astype(BF16)
+        cols = pl.ds(2 * half * W, 2 * W)
         for k in (2, 1, 3):
-            c_x[p, k] = send(xs.at[owner_rows(k, p)], rows.at[owner_rows(0, p)], dev(xx=at_x(k)))
-        l_x[p] = local(xs.at[owner_rows(0, p)], rows.at[owner_rows(0, p)])
+            send(xs.at[owner_rows(k, p), cols], rows.at[owner_rows(0, p), cols], dev(xx=at_x(k)), s_x[p])
+        if half == 1:
+            l_x[p] = local(xs.at[owner_rows(0, p)], rows.at[owner_rows(0, p)])
 
     c_fw = {}
 
     def forward(p):
+        rows = chunk(rows2, rows1, p)
         l_x[p].wait()
-        for k in (1, 3, 2):
-            c_x[p, k].wait_recv()
-        c_fw[p] = send(chunk(rows2, rows1, p), chunk(rsib2, rsib1, p), sibling)
+        arrived(s_x[p], rows.at[pl.ds(0, 3 * per_owner(p))])
+        c_fw[p] = send(rows, chunk(rsib2, rsib1, p), sibling)
 
     def swiglu(m, own, sib, weights):
         def up(n, carry):
@@ -354,15 +368,23 @@
             t = dot_nn(hbuf[0:m, :], dn[:, pl.ds(col(rel, c), W)])
             town[:, rel * W : (rel + 1) * W] = t.astype(BF16)
 
-    c_ret = {}
+    s_ret = {}
     l_ret = {}
 
     def give_back(p):
         town, rt = chunk(town2, town1, p), chunk(rt2, rt1, p)
+        trcv = chunk(trcv2, trcv1, p)
         c_t[p].wait_recv()
-        town[...] = (town[...].astype(F32) + chunk(trcv2, trcv1, p)[...].astype(F32)).astype(BF16)
-        for k in (2, 1, 3):
-            c_ret[p, k] = send(town.at[owner_rows(k, p)], rt.at[owner_rows(0, p)], dev(xx=at_x(k)))
+        for half in (1, 0):
+            cols = slice(2 * half * W, 2 * (half + 1) * W)
+            window = pl.ds(2 * half * W, 2 * W)
+            town[:, cols] = (town[:, cols].astype(F32) + trcv[:, cols].astype(F32)).astype(BF16)
+            s_ret[p, half] = group()
+            for k in (2, 1, 3):
+                send(
+                    town.at[owner_rows(k, p), window], rt.at[owner_rows(0, p), window],
+                    dev(xx=at_x(k)), s_ret[p, half],
+                )
         l_ret[p] = local(town.at[owner_rows(0, p)], rt.at[owner_rows(0, p)])
 
     c_y = {}
@@ -370,10 +392,12 @@
     def combine(p):
         wm, rt = chunk(wmat2, wmat1, p), chunk(rt2, rt1, p)
         l_ret[p].wait()
-        for k in (1, 3, 2):
-            c_ret[p, k].wait_recv()
         for rel in (2, 3, 1, 0):
-            for i, k in enumerate(BLOCKS[p]):
+            if rel in (1, 2):
+                half = rel // 2
+                arrived(s_ret[p, half], rt.at[pl.ds(0, 3 * per_owner(p)), pl.ds(2 * half * W, 2 * W)])
+            order = list(enumerate(BLOCKS[p]))
+            for i, k in order if rel in (2, 1) else order[::-1]:
                 got = dot_nn(wm[i * T : (i + 1) * T, :], rt[:, rel * W : (rel + 1) * W])
                 if k == 0:
                     got = got + sh_own[rel] + sh_r[rel].astype(F32)
@@ -386,8 +410,18 @@
                     ysnd[k, 1] = got.astype(BF16)
                     c_y[k, 0] = send(ysnd.at[k, 1], yrcv.at[k, 0], y_down)
 
-    build_slots(0)
-    slots(0)
+    def wait_y(p):
+        k = BLOCKS[p][0]
+        arrived(s_yfw[p], nb.at[k] if p < 4 else nb.at[k, pl.ds(0, 2)])
+
+    slots(0, 0)
+    for rel in (3, 2):
+        normalise(rel)
+    c_sib = send(nb.at[0], nsib, sibling)
+    slots(0, 1)
+    arrived(s_code, cz.at[pl.ds(1, NZ - 1)])
+    for p in (1, 2, 3, 4):
+        build_slots(p)
     l_router.wait()
     c_sib.wait_recv()
     logits = None
@@ -402,51 +436,47 @@
     sel_c = lax.broadcasted_iota(jnp.int32, (experts, experts), 1)
     sel_w = 2 * ((sel_r & 3) * NZ + (sel_r >> 3)) + ((sel_r >> 2) & 1)
     gt[...] = dot_nn(jnp.where(sel_c == sel_w, 1.0, 0.0).astype(BF16), gates)
-    c_gate = {}
+    s_gate = group()
     for k in range(1, NZ):
-        c_gate[k] = send(gt.at[pl.ds(pl.multiple_of(at_z(k) * 8, 8), 8)], gz.at[k], dev(zz=at_z(k)))
+        send(gt.at[pl.ds(pl.multiple_of(at_z(k) * 8, 8), 8)], gz.at[k], dev(zz=at_z(k)), s_gate)
     gz[0] = gt[pl.ds(pl.multiple_of(z * 8, 8), 8), :]
 
-    def wait_y(p):
-        for k in BLOCKS[p]:
-            yfw[k, 2].wait_recv()
-            yfw[k, 3].wait_recv()
-
-    for p in (1, 2, 3, 4):
-        build_slots(p)
     ring_step(0)
+    slots(1, 0)
+    forward(0)
     l_sg.wait()
     l_su.wait()
     l_sd.wait()
     swiglu(T, lambda rel: nb[0, rel], lambda rel: nsib[rel], sgu)
+    wait_y(1)
+    slots(1, 1)
+    ring_step(1)
+    slots(2, 0)
     for rel in range(4):
         sh_s[rel] = dot_nn(hbuf[0:T, :], sdn[:, pl.ds(col(rel, sc), W)]).astype(BF16)
     c_sh = send(sh_s, sh_r, sibling)
     for rel in range(4):
         sh_own[rel] = dot_nn(hbuf[0:T, :], sdn[:, pl.ds(col(rel, c), W)])
-    forward(0)
-    wait_y(1)
-    slots(1)
-    ring_step(1)
-    for p in (0, 1):
-        build_weights(p)
-    wait_y(2)
-    slots(2)
     l_g.wait()
     l_u.wait()
     l_d.wait()
     expert(0)
+    wait_y(2)
+    slots(2, 1)
     ring_step(2)
+    slots(3, 0)
     forward(1)
+    ring_step(3)
     wait_y(3)
-    slots(3)
+    slots(3, 1)
+    wait_y(4)
+    slots(4, 0)
+    slots(4, 1)
+    give_back(0)
     expert(1)
-    ring_step(3)
-    wait_y(4)
-    slots(4)
-    give_back(0)
     forward(2)
-    for p in (2, 3, 4):
+    arrived(s_gate, gz.at[pl.ds(1, NZ - 1)])
+    for p in range(5):
         build_weights(p)
     expert(2)
     forward(3)
@@ -481,7 +511,7 @@
         combine(4 - s)
         for ch in (1, 0):
             pass_on(0, "L", s, ch, 4 - s, z_left)
-            pass_on(1, "R", s, ch, 4 + s, z_right)
+            pass_on(1, "R", s, 1 - ch, 4 + s, z_right)
 
     def finish(ch):
         v = value(0, ch)
@@ -500,11 +530,12 @@
     q_s[...] = squares(wide)
     inv2 = inverse(share(q_s, q_r), q_s, q_r)
     out_n[...] = (wide * inv2 * gain_row(ngain, 0)).astype(BF16)
-    for cp in copies:
+    for cp in copies[-N_SEND:]:
         cp.wait_send()
 
 
-N_SEND = 192
+N_SEND = 32
+N_RECV = 94
 
 
 def on_device(
@@ -537,7 +568,7 @@
         vm((2, 4, 2, T, W), BF16), vm((2, 4, 2, T, W), BF16),
         vm((T, W), BF16), vm((T, W), BF16), vm((8, T), F32), vm((7, 8, T), F32),
         pltpu.SemaphoreType.DMA((13,)), pltpu.SemaphoreType.DMA((10,)),
-        pltpu.SemaphoreType.DMA((N_SEND,)), pltpu.SemaphoreType.DMA((N_SEND,)),
+        pltpu.SemaphoreType.DMA((N_SEND,)), pltpu.SemaphoreType.DMA((N_RECV,)),
     ]
     hbm = pl.BlockSpec(memory_space=pl.ANY)
     return pl.pallas_call(

time: 141 us -> 132 us (0.936)
  Pallas kernels: 137 us -> 127 us
    pallas_call x1, Pallas kernels: 137 us -> 127 us  [on_device(): pl.pallas_call(kernel, out_shape=(jax.ShapeDtypeStruct((T, W), BF16), jax...]
where the time goes in v3:
time: 132 us; the launch traced here: 131 us
  Pallas kernels  127 us (96%)
  local copies, waits for them, and re-layouts  3.14 us (2%)
    pallas_call x1, Pallas kernels, on_device(): pl.pallas_call(kernel, out_shape=(jax.ShapeDtypeStruct((T, W), BF16), jax...  127 us
    unnamed x2, local copies, waits for them, and re-layouts  3.14 us

profile of v3, /device:TPU:1, one launch (start us, length us, event | category | flops | bytes accessed | tf_op | source)
XLA Modules:
  0.0 131.4 jit_solution(1345278571793938153)
XLA Ops:
  1.3 127.0 %shard_map.131 = (bf16[256,256]{1,0:T(8,128)(2,1)}, bf16[256,256]{1,0:T(8,128)(2,1)}) custom-call(s32[1]{0:T(128)S(6)} %copy.16.live_ref, bf16[256,256]{1,0:T(8,128)(2,1)} %attn_h.1, bf16[256,2048]{1,0:T(8,128)(2,1)} %proj_h.1, bf16[256,2048]{1,0:T(8,128)(2,1)} %resid_h.1, f32[2048]{0:T(1024)} %gain_h.1, bf16[64,2048]{1,0:T(8,128)(2,1)} %bitcast.2, ...), custom_call_target="tpu_custom_call" | custom-call | tf_op jit(solution)/shard_map/pallas_call | solution.py:574
  128.3 1.6 %copy.17 = bf16[256,256]{1,0:T(8,128)(2,1)} copy(bf16[256,256]{1,0:T(8,128)(2,1)} %get-tuple-element.4) | data formatting | bytes 262144
  129.8 1.6 %copy.18 = bf16[256,256]{1,0:T(8,128)(2,1)} copy(bf16[256,256]{1,0:T(8,128)(2,1)} %get-tuple-element.5) | data formatting | bytes 262144

commit v4 on v3

--- a/solution.py
+++ b/solution.py
@@ -139,6 +139,7 @@
     peers += [dev(yy=at_y(k), cc=sc) for k in (1, 2, 3)]
     peers += [dev(xx=at_x(k)) for k in (1, 2, 3)]
     peers += [dev(zz=at_z(k)) for k in range(1, NZ)]
+    peers += [dev(zz=at_z(k), yy=at_y(j)) for k in (1, NZ - 1) for j in (1, NY - 1)]
     barrier = pltpu.get_barrier_semaphore()
     for peer in peers:
         pl.semaphore_signal(barrier, inc=1, device_id=peer, device_id_type=MESH)
@@ -371,11 +372,12 @@
     s_ret = {}
     l_ret = {}
 
-    def give_back(p):
+    def give_back(p, halves=(1, 0)):
         town, rt = chunk(town2, town1, p), chunk(rt2, rt1, p)
         trcv = chunk(trcv2, trcv1, p)
-        c_t[p].wait_recv()
-        for half in (1, 0):
+        if 1 in halves:
+            c_t[p].wait_recv()
+        for half in halves:
             cols = slice(2 * half * W, 2 * (half + 1) * W)
             window = pl.ds(2 * half * W, 2 * W)
             town[:, cols] = (town[:, cols].astype(F32) + trcv[:, cols].astype(F32)).astype(BF16)
@@ -385,16 +387,18 @@
                     town.at[owner_rows(k, p), window], rt.at[owner_rows(0, p), window],
                     dev(xx=at_x(k)), s_ret[p, half],
                 )
-        l_ret[p] = local(town.at[owner_rows(0, p)], rt.at[owner_rows(0, p)])
+            l_ret[p, half] = local(town.at[owner_rows(0, p), window], rt.at[owner_rows(0, p), window])
 
     c_y = {}
 
-    def combine(p):
+    def combine(p, halves=(1, 0)):
         wm, rt = chunk(wmat2, wmat1, p), chunk(rt2, rt1, p)
-        l_ret[p].wait()
         for rel in (2, 3, 1, 0):
+            if rel // 2 not in halves:
+                continue
             if rel in (1, 2):
                 half = rel // 2
+                l_ret[p, half].wait()
                 arrived(s_ret[p, half], rt.at[pl.ds(0, 3 * per_owner(p)), pl.ds(2 * half * W, 2 * W)])
             order = list(enumerate(BLOCKS[p]))
             for i, k in order if rel in (2, 1) else order[::-1]:
@@ -469,26 +473,28 @@
     ring_step(3)
     wait_y(3)
     slots(3, 1)
+    expert(1)
     wait_y(4)
     slots(4, 0)
     slots(4, 1)
     give_back(0)
-    expert(1)
     forward(2)
     arrived(s_gate, gz.at[pl.ds(1, NZ - 1)])
     for p in range(5):
         build_weights(p)
     expert(2)
+    give_back(1, (1,))
     forward(3)
-    expert(3)
     forward(4)
     expert(4)
+    expert(3)
     give_back(4)
     give_back(3)
     give_back(2)
-    give_back(1)
+    give_back(1, (0,))
     c_sh.wait_recv()
     combine(0)
+    combine(1, (1,))
 
     back = {}
 
@@ -504,27 +510,27 @@
         rs_s[wi, s, ch] = v.astype(BF16)
         back[way, s, ch] = send(rs_s.at[wi, s, ch], rs_r.at[wi, s, ch], to)
 
+    last_left = dev(zz=at_z(NZ - 1), yy=at_y(1))
+    last_right = dev(zz=at_z(1), yy=at_y(1))
     combine(4)
     pass_on(0, "L", 0, 0, 4, z_left)
     pass_on(1, "R", 0, 1, 4, z_right)
     for s in (1, 2, 3):
-        combine(4 - s)
+        if s == 2:
+            fb_s[...] = value(0, 1).astype(BF16)
+            c_fb = send(fb_s, fb_r, y_up)
+        combine(4 - s, (1, 0) if s < 3 else (0,))
         for ch in (1, 0):
-            pass_on(0, "L", s, ch, 4 - s, z_left)
-            pass_on(1, "R", s, 1 - ch, 4 + s, z_right)
-
-    def finish(ch):
-        v = value(0, ch)
-        for wi, way in ((0, "L"), (1, "R")):
-            back[way, 3, ch].wait_recv()
-            v = v + rs_r[wi, 3, ch].astype(F32)
-        return v
-
-    fb_s[...] = finish(1).astype(BF16)
-    c_fb = send(fb_s, fb_r, y_up)
-    mine = finish(0) + st[0].astype(F32)
+            pass_on(0, "L", s, ch, 4 - s, last_left if s == 3 and ch == 1 else z_left)
+            pass_on(1, "R", s, 1 - ch, 4 + s, last_right if s == 3 and ch == 0 else z_right)
+
+    mine = value(0, 0) + st[0].astype(F32)
     c_fb.wait_recv()
-    nxt = (mine + fb_r[...].astype(F32)).astype(BF16)
+    mine = mine + fb_r[...].astype(F32)
+    for wi, way, ch in ((0, "L", 1), (1, "R", 0), (0, "L", 0), (1, "R", 1)):
+        back[way, 3, ch].wait_recv()
+        mine = mine + rs_r[wi, 3, ch].astype(F32)
+    nxt = mine.astype(BF16)
     out_s[...] = nxt
     wide = nxt.astype(F32)
     q_s[...] = squares(wide)
@@ -567,7 +573,7 @@
         vm((NZ, 2, T, W), F32), vm((NZ, 2, T, W), BF16), vm((NZ, 2, T, W), BF16),
         vm((2, 4, 2, T, W), BF16), vm((2, 4, 2, T, W), BF16),
         vm((T, W), BF16), vm((T, W), BF16), vm((8, T), F32), vm((7, 8, T), F32),
-        pltpu.SemaphoreType.DMA((13,)), pltpu.SemaphoreType.DMA((10,)),
+        pltpu.SemaphoreType.DMA((13,)), pltpu.SemaphoreType.DMA((15,)),
         pltpu.SemaphoreType.DMA((N_SEND,)), pltpu.SemaphoreType.DMA((N_RECV,)),
     ]
     hbm = pl.BlockSpec(memory_space=pl.ANY)

time: 132 us -> 132 us (level); the launches traced: 131 us -> 130 us
    pallas_call x1, Pallas kernels: 127 us -> 126 us  [on_device(): pl.pallas_call(kernel, out_shape=(jax.ShapeDtypeStruct((T, W), BF16), jax...]
where the time goes in v4:
time: 132 us; the launch traced here: 130 us
  Pallas kernels  126 us (95%)
  local copies, waits for them, and re-layouts  3.14 us (2%)
    pallas_call x1, Pallas kernels, on_device(): pl.pallas_call(kernel, out_shape=(jax.ShapeDtypeStruct((T, W), BF16), jax...  126 us
    unnamed x2, local copies, waits for them, and re-layouts  3.14 us

profile of v4, /device:TPU:1, one launch (start us, length us, event | category | flops | bytes accessed | tf_op | source)
XLA Modules:
  0.0 130.0 jit_solution(17335865134813824257)
XLA Ops:
  1.3 125.6 %shard_map.131 = (bf16[256,256]{1,0:T(8,128)(2,1)}, bf16[256,256]{1,0:T(8,128)(2,1)}) custom-call(s32[1]{0:T(128)S(6)} %copy.16.live_ref, bf16[256,256]{1,0:T(8,128)(2,1)} %attn_h.1, bf16[256,2048]{1,0:T(8,128)(2,1)} %proj_h.1, bf16[256,2048]{1,0:T(8,128)(2,1)} %resid_h.1, f32[2048]{0:T(1024)} %gain_h.1, bf16[64,2048]{1,0:T(8,128)(2,1)} %bitcast.2, ...), custom_call_target="tpu_custom_call" | custom-call | tf_op jit(solution)/shard_map/pallas_call | solution.py:580
  126.9 1.6 %copy.17 = bf16[256,256]{1,0:T(8,128)(2,1)} copy(bf16[256,256]{1,0:T(8,128)(2,1)} %get-tuple-element.4) | data formatting | bytes 262144
  128.4 1.6 %copy.18 = bf16[256,256]{1,0:T(8,128)(2,1)} copy(bf16[256,256]{1,0:T(8,128)(2,1)} %get-tuple-element.5) | data formatting | bytes 262144

commit v5 on v3

--- a/solution.py
+++ b/solution.py
@@ -525,11 +525,11 @@
     mine = finish(0) + st[0].astype(F32)
     c_fb.wait_recv()
     nxt = (mine + fb_r[...].astype(F32)).astype(BF16)
-    out_s[...] = nxt
     wide = nxt.astype(F32)
+    out_s[...] = wide
     q_s[...] = squares(wide)
     inv2 = inverse(share(q_s, q_r), q_s, q_r)
-    out_n[...] = (wide * inv2 * gain_row(ngain, 0)).astype(BF16)
+    out_n[...] = inv2 * gain_row(ngain, 0)
     for cp in copies[-N_SEND:]:
         cp.wait_send()
 
@@ -571,9 +571,9 @@
         pltpu.SemaphoreType.DMA((N_SEND,)), pltpu.SemaphoreType.DMA((N_RECV,)),
     ]
     hbm = pl.BlockSpec(memory_space=pl.ANY)
-    return pl.pallas_call(
+    stream, scale = pl.pallas_call(
         kernel,
-        out_shape=(jax.ShapeDtypeStruct((T, W), BF16), jax.ShapeDtypeStruct((T, W), BF16)),
+        out_shape=(jax.ShapeDtypeStruct((T, W), F32), jax.ShapeDtypeStruct((T, W), F32)),
         in_specs=[pl.BlockSpec(memory_space=pltpu.SMEM)] + [hbm] * 11,
         out_specs=(pl.BlockSpec(memory_space=pltpu.VMEM), pl.BlockSpec(memory_space=pltpu.VMEM)),
         scratch_shapes=scratch,
@@ -584,6 +584,7 @@
         live_rows, attn_out, out_proj, residual, norm_gain, router.T, expert_gate_up,
         expert_down, shared_gate_up, shared_down, routes.T, next_gain,
     )
+    return stream.astype(BF16), (stream * scale).astype(BF16)
 
 
 def solution(mesh):

time: 132 us -> 130 us (0.985)
  local copies, waits for them, and re-layouts: 3.14 us -> 0 us
  other arithmetic: 0 us -> 1.85 us
    unnamed x2 -> x0, local copies, waits for them, and re-layouts: 3.14 us -> none
    convert_element_type x0 -> x1, other arithmetic: none -> 1.85 us  [on_device(): return (stream.astype(BF16), (stream * scale).astype(BF16))]
where the time goes in v5:
time: 130 us
  Pallas kernels  127 us (98%)
  other arithmetic  1.85 us (1%)
    pallas_call x1, Pallas kernels, on_device(): pl.pallas_call(kernel, out_shape=(jax.ShapeDtypeStruct((T, W), F32), jax....  127 us

profile of v5, /device:TPU:1, one launch (start us, length us, event | category | flops | bytes accessed | tf_op | source)
XLA Modules:
  0.0 130.2 jit_solution(6489082451299677685)
XLA Ops:
  1.3 127.0 %shard_map.131 = (f32[256,256]{1,0:T(8,128)}, f32[256,256]{1,0:T(8,128)}) custom-call(s32[1]{0:T(128)S(6)} %copy.14.live_ref, bf16[256,256]{1,0:T(8,128)(2,1)} %attn_h.1, bf16[256,2048]{1,0:T(8,128)(2,1)} %proj_h.1, bf16[256,2048]{1,0:T(8,128)(2,1)} %resid_h.1, f32[2048]{0:T(1024)} %gain_h.1, bf16[64,2048]{1,0:T(8,128)(2,1)} %bitcast.2, ...), custom_call_target="tpu_custom_call" | custom-call | tf_op jit(solution)/shard_map/pallas_call | solution.py:574
  128.3 1.8 %multiply_convert_fusion = (bf16[256,256]{1,0:T(8,128)(2,1)}, bf16[256,256]{1,0:T(8,128)(2,1)}) fusion(f32[256,256]{1,0:T(8,128)} %get-tuple-element.4, f32[256,256]{1,0:T(8,128)} %get-tuple-element.5), kind=kLoop, calls=%fused_computation | loop fusion | flops 196608 | bytes 786432 | tf_op jit(solution)/shard_map/convert_element_type | solution.py:587

commit v6 on v5

--- a/solution.py
+++ b/solution.py
@@ -511,7 +511,7 @@
         combine(4 - s)
         for ch in (1, 0):
             pass_on(0, "L", s, ch, 4 - s, z_left)
-            pass_on(1, "R", s, 1 - ch, 4 + s, z_right)
+            pass_on(1, "R", s, 1 - ch if s < 3 else ch, 4 + s, z_right)
 
     def finish(ch):
         v = value(0, ch)

time: 130 us -> 130 us (level)
  no operation moved by 1% of the time
where the time goes in v6:
time: 130 us
  Pallas kernels  126 us (97%)
  other arithmetic  1.85 us (1%)
    pallas_call x1, Pallas kernels, on_device(): pl.pallas_call(kernel, out_shape=(jax.ShapeDtypeStruct((T, W), F32), jax....  126 us

profile of v6, /device:TPU:1, one launch (start us, length us, event | category | flops | bytes accessed | tf_op | source)
XLA Modules:
  0.0 129.6 jit_solution(1312224235399169302)
XLA Ops:
  1.3 126.4 %shard_map.131 = (f32[256,256]{1,0:T(8,128)}, f32[256,256]{1,0:T(8,128)}) custom-call(s32[1]{0:T(128)S(6)} %copy.14.live_ref, bf16[256,256]{1,0:T(8,128)(2,1)} %attn_h.1, bf16[256,2048]{1,0:T(8,128)(2,1)} %proj_h.1, bf16[256,2048]{1,0:T(8,128)(2,1)} %resid_h.1, f32[2048]{0:T(1024)} %gain_h.1, bf16[64,2048]{1,0:T(8,128)(2,1)} %bitcast.2, ...), custom_call_target="tpu_custom_call" | custom-call | tf_op jit(solution)/shard_map/pallas_call | solution.py:574
  127.7 1.8 %multiply_convert_fusion = (bf16[256,256]{1,0:T(8,128)(2,1)}, bf16[256,256]{1,0:T(8,128)(2,1)}) fusion(f32[256,256]{1,0:T(8,128)} %get-tuple-element.4, f32[256,256]{1,0:T(8,128)} %get-tuple-element.5), kind=kLoop, calls=%fused_computation | loop fusion | flops 196608 | bytes 786432 | tf_op jit(solution)/shard_map/convert_element_type | solution.py:587
